TPU v7x, 256 devices: a whole 4x4x8 slice. The times are simulated.
256 devices in a mesh: grp: 32 (over z_lo, x, core), slab: 8 (over z_hi, y).
Axes of the slice: x: 4, y: 4, z: 8 (z_hi: 2, z_lo: 4; z = z_hi * 4 + z_lo), core: 2. Of those that a mesh axis runs over, the one named last changes fastest.
Arguments:
- fwd_fields: float32 [32, 6, 64, 128, 128], P('grp', None, 'slab'), may hold values from -6 to 6
- adj_fields: float32 [32, 6, 64, 128, 128], P('grp', None, 'slab'), may hold values from -6 to 6
- density: float32 [64, 128, 128], P('slab', 'grp'), may hold values from 0 to 1
- block_ids: int32 [32], replicated, may hold values from 0 to 31, each once
- material_idx: int32 [32], replicated, may hold values from 0 to 3
- material_eps: float32 [4], replicated, may hold values from 1 to 12
- source_pos: int32 [32, 3], P('grp'), may hold values from 0 to 127, as said below
- wave_idx: int32 [32], P('grp'), may hold values from 0 to 3
Outputs:
- final_fields: float32 [32, 6, 64, 128, 128], P('grp', None, 'slab')
- grad_density: float32 [64, 128, 128], P('slab', 'grp')
Inputs may be any that keep to these rules, and one draw needn't show every extreme that they name: `block_ids`: a permutation of the 32 blocks. `source_pos`: cells inside the window: z below 64, x below 128, y below 128; some group's z is 0, some group's x is 127 and some group's y is 127.
All inputs are finite; a program needn't handle non-finite values.
Results may differ from a plain program's by a relative error of at most 0.0003.
Values sent between devices are 32-bit elements; how exact they have to be, the bound alone decides.
A program may use at most 64 MiB of HBM per device.

v0:
```python
import math

import jax
import jax.numpy as jnp
from jax import lax
from jax.sharding import PartitionSpec as P

STEPS = 4


COURANT = 0.5
AMPLITUDE = 4.0


def from_everyone(shard, axis):
    copies = jnp.broadcast_to(shard, (lax.axis_size(axis), *shard.shape))
    return lax.all_to_all(copies, axis, split_axis=0, concat_axis=0, tiled=True)


def joined_along(pieces, dim):
    pieces = jnp.moveaxis(pieces, 0, dim)
    dims = pieces.shape
    return pieces.reshape(*dims[:dim], dims[dim] * dims[dim + 1], *dims[dim + 2 :])


def gathered_copies(shard, axis, dim):
    pieces = from_everyone(shard, axis)
    return joined_along(pieces, dim)


def from_behind(block, axis, distance):
    devices = range(lax.axis_size(axis))
    route = [(i - distance, i) for i in devices if i - distance in devices]
    return lax.ppermute(block, axis, route)


def split_up(shard, dim, count):
    dims = shard.shape
    pieces = shard.reshape(*dims[:dim], count, dims[dim] // count, *dims[dim + 1 :])
    return jnp.moveaxis(pieces, dim, 0)


def sum_at_owner(shard, axis, dim):
    pieces = split_up(shard, dim, lax.axis_size(axis))
    arrived = lax.all_to_all(pieces, axis, split_axis=0, concat_axis=0, tiled=True)
    return arrived.sum(axis=0)


def fwd_diff(field, axis):
    pads = [(0, 0)] * field.ndim
    pads[axis] = (0, 1)
    padded = jnp.pad(field, pads)
    return lax.slice_in_dim(padded, 1, field.shape[axis] + 1, axis=axis) - field


def bwd_diff(field, axis):
    pads = [(0, 0)] * field.ndim
    pads[axis] = (1, 0)
    padded = jnp.pad(field, pads)
    return field - lax.slice_in_dim(padded, 0, field.shape[axis], axis=axis)


def above_diff(field, upper):
    return jnp.concatenate([field[:, 1:], upper], axis=1) - field


def below_diff(field, lower):
    return field - jnp.concatenate([lower, field[:, :-1]], axis=1)


def filter_xy(values):
    padded = jnp.pad(values, ((0, 0), (1, 1), (1, 1)))
    rows = padded[:, :-2] + 2.0 * padded[:, 1:-1] + padded[:, 2:]
    return (rows[:, :, :-2] + 2.0 * rows[:, :, 1:-1] + rows[:, :, 2:]) / 16.0


def source_profile(zcoord, xcoord, ycoord, position, width_x, width_y):
    in_plane = (zcoord == position[0]).astype(jnp.float32)
    offset_x = (xcoord - position[1]).astype(jnp.float32) / (width_x / 4.0)
    offset_y = (ycoord - position[2]).astype(jnp.float32) / (width_y / 4.0)
    return in_plane * jnp.exp(-0.5 * (offset_x * offset_x + offset_y * offset_y))


def layer_grid(first, layers, width_x, width_y):
    shape = (layers, width_x, width_y)
    zcoord = lax.broadcasted_iota(jnp.int32, shape, 0) + first
    xcoord = lax.broadcasted_iota(jnp.int32, shape, 1)
    ycoord = lax.broadcasted_iota(jnp.int32, shape, 2)
    return (zcoord, xcoord, ycoord)


def per_device(
    fwd_fields, adj_fields, density, block_ids, material_idx, material_eps, source_pos, wave_idx
):
    depth = fwd_fields.shape[2]
    width_x = fwd_fields.shape[3]
    width_y = fwd_fields.shape[4]
    nblock = block_ids.shape[0]
    block_rows = width_x // nblock
    slab_first = lax.axis_index("slab") * depth
    owned = gathered_copies(density, "grp", 1)
    blocks = owned.reshape(depth, nblock, block_rows, width_y)
    placed = jnp.zeros_like(blocks).at[:, block_ids].set(blocks).reshape(depth, width_x, width_y)
    smooth = filter_xy(placed)
    onehot = (
        material_idx[:, None] == jnp.arange(material_eps.shape[0], dtype=jnp.int32)[None, :]
    ).astype(jnp.float32)
    base = jnp.sum(onehot * material_eps[None, :], axis=1)
    base_rows = jnp.repeat(base, block_rows)
    eps = base_rows[None, :, None] + 3.0 * smooth
    coef = 0.5 / eps
    position = source_pos[0]
    omega = 2.0 * math.pi / (6.0 + 2.0 * wave_idx[0].astype(jnp.float32))
    comps = [jnp.stack([fwd_fields[0, c], adj_fields[0, c]]) for c in range(6)]
    ex, ey, ez, hx, hy, hz = comps
    intersections = []
    zcoord, xcoord, ycoord = layer_grid(slab_first, depth, width_x, width_y)
    profile = source_profile(zcoord, xcoord, ycoord, position, width_x, width_y)
    zeros_field = jnp.zeros_like(profile)
    for step in range(STEPS):
        upper = from_behind(jnp.stack([ex[:, :1], ey[:, :1]]), "slab", -1)
        hx = hx - COURANT * (fwd_diff(ez, 3) - above_diff(ey, upper[1]))
        hy = hy - COURANT * (above_diff(ex, upper[0]) - fwd_diff(ez, 2))
        hz = hz - COURANT * (fwd_diff(ey, 2) - fwd_diff(ex, 3))
        lower = from_behind(jnp.stack([hx[:, -1:], hy[:, -1:]]), "slab", 1)
        drive = jnp.stack([AMPLITUDE * jnp.sin(omega * (step + 1.0)) * profile, zeros_field])
        ex = ex + coef * (bwd_diff(hz, 3) - below_diff(hy, lower[1]))
        ey = ey + coef * (below_diff(hx, lower[0]) - bwd_diff(hz, 2))
        ez = ez + coef * (bwd_diff(hy, 2) - bwd_diff(hx, 3)) + drive
        intersections.append(ex[0] * ex[1] + ey[0] * ey[1] + ez[0] * ez[1])
    total = intersections[0]
    for intersection in intersections[1:]:
        total = total + intersection
    grad_sum = sum_at_owner(
        filter_xy(total)
        .reshape(depth, nblock, block_rows, width_y)[:, block_ids]
        .reshape(depth, width_x, width_y),
        "grp",
        1,
    )
    scale = 3.0 / (STEPS * math.sqrt(lax.axis_size("grp")))
    finals = jnp.stack([ex[0], ey[0], ez[0], hx[0], hy[0], hz[0]])[None]
    return (finals, grad_sum * scale)


def solution(mesh):
    placed = (
        P("grp", None, "slab", None, None),
        P("grp", None, "slab", None, None),
        P("slab", "grp", None),
        P(),
        P(),
        P(),
        P("grp", None),
        P("grp"),
    )
    return jax.shard_map(
        per_device,
        mesh=mesh,
        in_specs=placed,
        out_specs=(P("grp", None, "slab", None, None), P("slab", "grp", None)),
        check_vma=False,
    )
```

profile of v0, /device:TPU:25, one launch (start us, length us, event | category | flops | bytes accessed | tf_op | source)
XLA Modules:
  0.0 180.8 jit_solution(8764324955699824154)
XLA Ops:
  0.6 3.2 %slice_bitcast_fusion = (f32[1,8,128,128]{3,2,1,0:T(8,128)}, f32[1,8,128,128]{3,2,1,0:T(8,128)}, f32[1,8,128,128]{3,2,1,0:T(8,128)S(1)}, f32[1,8,128,128]{3,2,1,...) fusion(f32[1,6,8,128,128]{4,3,2,1,0:T(8,128)} %param.9), kind=kLoop, calls=%fused_computation.223 | loop fusion | bytes 6291456 | tf_op jit(solution)/shard_map/stack;squeeze | solution.py:114
  6.0 2.4 %collective-permute-start = (f32[2,2,1,128,128]{4,3,1,2,0:T(8,128)}, f32[2,2,1,128,128]{4,3,1,2,0:T(8,128)S(1)}, u32[]{:S(2)}, u32[]{:S(2)}) collective-permute-start(f32[2,2,1,128,128]{4,3,1,2,0:T(8,128)} %pad_maximum_fusion.3), channel_id=1, source_target_pairs={{1,0},{2,1},{3,2},{4,3},{5,4},{6,5},{7,6},{9,8},{10,9},{11,10},{12... | collective-permute-start | bytes 786440 | tf_op jit(solution)/shard_map/ppermute | solution.py:34
  9.3 9.5 %all-to-all-start = ((f32[32,8,4,128]{3,1,2,0:T(8,128)}), f32[32,8,4,128]{3,1,2,0:T(8,128)}, u32[]{:S(2)}, u32[]{:S(2)}) async-start(f32[32,8,4,128]{3,1,2,0:T(8,128)} %broadcast_in_dim.13), calls=%async_computation | async-start | bytes 1048576 | tf_op jit(solution)/shard_map/all_to_all | solution.py:17
  26.4 1.6 fusion.132
  33.3 9.1 %collective-permute-start.1 = (f32[2,2,1,128,128]{4,3,1,2,0:T(8,128)S(1)}, f32[2,2,1,128,128]{4,3,1,2,0:T(8,128)S(1)}, u32[]{:S(2)}, u32[]{:S(2)}) collective-permute-start(f32[2,2,1,128,128]{4,3,1,2,0:T(8,128)S(1)} %pad_maximum_fusion.4), channel_id=1, source_target_pairs={{0,1},{1,2},{2,3},{3,4},{4,5},{5,6},{6,7},{8,9},{9,10},{10,11},{11... | collective-permute-start | bytes 786440 | tf_op jit(solution)/shard_map/ppermute | solution.py:34
  44.8 2.9 %collective-permute-done.1 = f32[2,2,1,128,128]{4,3,1,2,0:T(8,128)S(1)} collective-permute-done((f32[2,2,1,128,128]{4,3,1,2,0:T(8,128)S(1)}, f32[2,2,1,128,128]{4,3,1,2,0:T(8,128)S(1)}, u32[]{:S(2)}, u32[]{:S(2)}) %collective-permute-start.1) | collective-permute-done | bytes 262176 | tf_op jit(solution)/shard_map/ppermute | solution.py:34
  48.6 4.8 %scatter_fusion = f32[8,32,4,128]{3,0,2,1:T(8,128)} fusion(f32[8,32,4,128]{3,0,2,1:T(8,128)} %broadcast_in_dim.11, s32[32]{0:T(128)S(1)} %compare_select_fusion, f32[32,8,4,128]{3,1,2,0:T(8,128)} %all-to-all-done), kind=kCustom, calls=%fused_computation.1 | custom fusion | bytes 1572992 | tf_op jit(solution)/shard_map/scatter | solution.py:103
  56.7 2.6 %fusion.18 = (f32[2,8,128,128]{3,2,1,0:T(8,128)S(1)}, f32[2,8,128,128]{3,2,1,0:T(8,128)S(1)}, f32[2,8,128,128]{3,2,1,0:T(8,128)S(1)}) fusion(f32[2,8,128,128]{3,2,1,0:T(8,128)S(1)} %get-tuple-element.61, f32[2,8,128,128]{3,2,1,0:T(8,128)S(1)} %get-tuple-element.60, f32[1,8,128,128]{3,2,1,0:T(8,128)S(1)} %copy-done.30, f32[8,128,128]{2,1,0:T(8,128)S(1)} %fusion.130, ...), kind=kLoop, calls=%fused_computation.66 | loop fusion | flops 5242880 | bytes 12582912 | tf_op jit(solution)/shard_map/add | solution.py:129
  59.4 2.1 %collective-permute-start.2 = (f32[2,2,1,128,128]{4,3,1,2,0:T(8,128)S(1)}, f32[2,2,1,128,128]{4,3,1,2,0:T(8,128)S(1)}, u32[]{:S(2)}, u32[]{:S(2)}) collective-permute-start(f32[2,2,1,128,128]{4,3,1,2,0:T(8,128)S(1)} %pad_maximum_fusion.5), channel_id=1, source_target_pairs={{1,0},{2,1},{3,2},{4,3},{5,4},{6,5},{7,6},{9,8},{10,9},{11,10},{12... | collective-permute-start | bytes 786440 | tf_op jit(solution)/shard_map/ppermute | solution.py:34
  61.6 13.5 %collective-permute-done.2 = f32[2,2,1,128,128]{4,3,1,2,0:T(8,128)S(1)} collective-permute-done((f32[2,2,1,128,128]{4,3,1,2,0:T(8,128)S(1)}, f32[2,2,1,128,128]{4,3,1,2,0:T(8,128)S(1)}, u32[]{:S(2)}, u32[]{:S(2)}) %collective-permute-start.2) | collective-permute-done | bytes 262176 | tf_op jit(solution)/shard_map/ppermute | solution.py:34
  76.8 3.2 %collective-permute-start.3 = (f32[2,2,1,128,128]{4,3,1,2,0:T(8,128)S(1)}, f32[2,2,1,128,128]{4,3,1,2,0:T(8,128)S(1)}, u32[]{:S(2)}, u32[]{:S(2)}) collective-permute-start(f32[2,2,1,128,128]{4,3,1,2,0:T(8,128)S(1)} %pad_maximum_fusion.6), channel_id=1, source_target_pairs={{0,1},{1,2},{2,3},{3,4},{4,5},{5,6},{6,7},{8,9},{9,10},{10,11},{11... | collective-permute-start | bytes 786440 | tf_op jit(solution)/shard_map/ppermute | solution.py:34
  80.1 4.7 %collective-permute-done.3 = f32[2,2,1,128,128]{4,3,1,2,0:T(8,128)S(1)} collective-permute-done((f32[2,2,1,128,128]{4,3,1,2,0:T(8,128)S(1)}, f32[2,2,1,128,128]{4,3,1,2,0:T(8,128)S(1)}, u32[]{:S(2)}, u32[]{:S(2)}) %collective-permute-start.3) | collective-permute-done | bytes 262176 | tf_op jit(solution)/shard_map/ppermute | solution.py:34
  86.3 1.9 %collective-permute-start.4 = (f32[2,2,1,128,128]{4,3,1,2,0:T(8,128)S(1)}, f32[2,2,1,128,128]{4,3,1,2,0:T(8,128)S(1)}, u32[]{:S(2)}, u32[]{:S(2)}) collective-permute-start(f32[2,2,1,128,128]{4,3,1,2,0:T(8,128)S(1)} %pad_maximum_fusion.7), channel_id=1, source_target_pairs={{1,0},{2,1},{3,2},{4,3},{5,4},{6,5},{7,6},{9,8},{10,9},{11,10},{12... | collective-permute-start | bytes 786440 | tf_op jit(solution)/shard_map/ppermute | solution.py:34
  88.4 11.0 %collective-permute-done.4 = f32[2,2,1,128,128]{4,3,1,2,0:T(8,128)S(1)} collective-permute-done((f32[2,2,1,128,128]{4,3,1,2,0:T(8,128)S(1)}, f32[2,2,1,128,128]{4,3,1,2,0:T(8,128)S(1)}, u32[]{:S(2)}, u32[]{:S(2)}) %collective-permute-start.4) | collective-permute-done | bytes 262176 | tf_op jit(solution)/shard_map/ppermute | solution.py:34
  100.9 3.1 %collective-permute-start.5 = (f32[2,2,1,128,128]{4,3,1,2,0:T(8,128)S(1)}, f32[2,2,1,128,128]{4,3,1,2,0:T(8,128)S(1)}, u32[]{:S(2)}, u32[]{:S(2)}) collective-permute-start(f32[2,2,1,128,128]{4,3,1,2,0:T(8,128)S(1)} %pad_maximum_fusion.8), channel_id=1, source_target_pairs={{0,1},{1,2},{2,3},{3,4},{4,5},{5,6},{6,7},{8,9},{9,10},{10,11},{11... | collective-permute-start | bytes 786440 | tf_op jit(solution)/shard_map/ppermute | solution.py:34
  104.2 4.0 %collective-permute-done.5 = f32[2,2,1,128,128]{4,3,1,2,0:T(8,128)S(1)} collective-permute-done((f32[2,2,1,128,128]{4,3,1,2,0:T(8,128)S(1)}, f32[2,2,1,128,128]{4,3,1,2,0:T(8,128)S(1)}, u32[]{:S(2)}, u32[]{:S(2)}) %collective-permute-start.5) | collective-permute-done | bytes 262176 | tf_op jit(solution)/shard_map/ppermute | solution.py:34
  109.7 1.9 %collective-permute-start.6 = (f32[2,2,1,128,128]{4,3,1,2,0:T(8,128)S(1)}, f32[2,2,1,128,128]{4,3,1,2,0:T(8,128)S(1)}, u32[]{:S(2)}, u32[]{:S(2)}) collective-permute-start(f32[2,2,1,128,128]{4,3,1,2,0:T(8,128)S(1)} %pad_maximum_fusion.9), channel_id=1, source_target_pairs={{1,0},{2,1},{3,2},{4,3},{5,4},{6,5},{7,6},{9,8},{10,9},{11,10},{12... | collective-permute-start | bytes 786440 | tf_op jit(solution)/shard_map/ppermute | solution.py:34
  111.8 11.0 %collective-permute-done.6 = f32[2,2,1,128,128]{4,3,1,2,0:T(8,128)S(1)} collective-permute-done((f32[2,2,1,128,128]{4,3,1,2,0:T(8,128)S(1)}, f32[2,2,1,128,128]{4,3,1,2,0:T(8,128)S(1)}, u32[]{:S(2)}, u32[]{:S(2)}) %collective-permute-start.6) | collective-permute-done | bytes 262176 | tf_op jit(solution)/shard_map/ppermute | solution.py:34
  124.3 2.8 %collective-permute-start.7 = (f32[2,2,1,128,128]{4,3,1,2,0:T(8,128)S(1)}, f32[2,2,1,128,128]{4,3,1,2,0:T(8,128)S(1)}, u32[]{:S(2)}, u32[]{:S(2)}) collective-permute-start(f32[2,2,1,128,128]{4,3,1,2,0:T(8,128)S(1)} %pad_maximum_fusion.10), channel_id=1, source_target_pairs={{0,1},{1,2},{2,3},{3,4},{4,5},{5,6},{6,7},{8,9},{9,10},{10,11},{11... | collective-permute-start | bytes 786440 | tf_op jit(solution)/shard_map/ppermute | solution.py:34
  127.2 4.1 %collective-permute-done.7 = f32[2,2,1,128,128]{4,3,1,2,0:T(8,128)S(1)} collective-permute-done((f32[2,2,1,128,128]{4,3,1,2,0:T(8,128)S(1)}, f32[2,2,1,128,128]{4,3,1,2,0:T(8,128)S(1)}, u32[]{:S(2)}, u32[]{:S(2)}) %collective-permute-start.7) | collective-permute-done | bytes 262176 | tf_op jit(solution)/shard_map/ppermute | solution.py:34
  137.1 2.7 %gather_fusion = f32[32,8,4,128]{3,2,1,0:T(4,128)} fusion(f32[8,32,4,128]{3,2,1,0:T(4,128)} %bitcast.143, s32[1024]{0:T(1024)S(1)} %pad_clamp_fusion), kind=kCustom, calls=%fused_computation | custom fusion | bytes 1048704 | tf_op jit(solution)/shard_map/gather | solution.py:135
  139.8 22.7 %all-to-all-start.1 = ((f32[32,8,4,128]{3,2,1,0:T(4,128)}), f32[32,8,4,128]{3,2,1,0:T(4,128)}, u32[]{:S(2)}, u32[]{:S(2)}) async-start(f32[32,8,4,128]{3,2,1,0:T(4,128)} %gather_fusion), calls=%async_computation.1 | async-start | bytes 1048576 | tf_op jit(solution)/shard_map/all_to_all | solution.py:45
  162.6 2.0 %slice_dynamic-update-slice_fusion.4 = f32[6,8,128,128]{3,2,1,0:T(8,128)} fusion(f32[6,8,128,128]{3,2,1,0:T(8,128)} %slice_dynamic-update-slice_fusion.5, f32[2,8,128,128]{3,2,1,0:T(8,128)} %copy-done.6), kind=kLoop, calls=%fused_computation.236 | loop fusion | bytes 1048576
  167.8 11.2 %all-to-all-done.1 = f32[32,8,4,128]{3,2,1,0:T(4,128)} async-done(((f32[32,8,4,128]{3,2,1,0:T(4,128)}), f32[32,8,4,128]{3,2,1,0:T(4,128)}, u32[]{:S(2)}, u32[]{:S(2)}) %all-to-all-start.1) | async-done | bytes 524320 | tf_op jit(solution)/shard_map/all_to_all | solution.py:45
  (161 shorter events, 40.1 us)
Async XLA Ops:
  3.9 17.8 %copy-start.13 = (f32[1,8,128,128]{3,2,1,0:T(8,128)}, f32[1,8,128,128]{3,2,1,0:T(8,128)S(1)}, u32[]{:S(2)}) copy-start(f32[1,8,128,128]{3,2,1,0:T(8,128)S(1)} %get-tuple-element.13) | copy-start | bytes 1572868
  5.2 16.5 %copy-start.15 = (f32[1,8,128,128]{3,2,1,0:T(8,128)}, f32[1,8,128,128]{3,2,1,0:T(8,128)S(1)}, u32[]{:S(2)}) copy-start(f32[1,8,128,128]{3,2,1,0:T(8,128)S(1)} %get-tuple-element.7) | copy-start | bytes 1572868
  6.0 22.0 %collective-permute-start = (f32[2,2,1,128,128]{4,3,1,2,0:T(8,128)}, f32[2,2,1,128,128]{4,3,1,2,0:T(8,128)S(1)}, u32[]{:S(2)}, u32[]{:S(2)}) collective-permute-start(f32[2,2,1,128,128]{4,3,1,2,0:T(8,128)} %pad_maximum_fusion.3), channel_id=1, source_target_pairs={{1,0},{2,1},{3,2},{4,3},{5,4},{6,5},{7,6},{9,8},{10,9},{11,10},{12... | collective-permute-start | bytes 786440 | tf_op jit(solution)/shard_map/ppermute | solution.py:34
  9.3 38.4 %all-to-all-start = ((f32[32,8,4,128]{3,1,2,0:T(8,128)}), f32[32,8,4,128]{3,1,2,0:T(8,128)}, u32[]{:S(2)}, u32[]{:S(2)}) async-start(f32[32,8,4,128]{3,1,2,0:T(8,128)} %broadcast_in_dim.13), calls=%async_computation | async-start | bytes 1048576 | tf_op jit(solution)/shard_map/all_to_all | solution.py:17
  28.4 14.0 %copy-start.2 = (f32[2,8,128,128]{3,2,0,1:T(8,128)}, f32[2,8,128,128]{3,2,0,1:T(8,128)S(1)}, u32[]{:S(2)}) copy-start(f32[2,8,128,128]{3,2,0,1:T(8,128)S(1)} %get-tuple-element.36) | copy-start | bytes 3145732
  31.3 11.1 %copy-start.18 = (f32[2,8,128,128]{3,2,0,1:T(8,128)S(1)}, f32[2,8,128,128]{3,2,0,1:T(8,128)}, u32[]{:S(2)}) copy-start(f32[2,8,128,128]{3,2,0,1:T(8,128)} %copy.78) | copy-start | bytes 3145732
  33.3 10.4 %copy-start.9 = (f32[1,8,128,128]{3,2,1,0:T(8,128)S(1)}, f32[1,8,128,128]{3,2,1,0:T(8,128)}, u32[]{:S(2)}) copy-start(f32[1,8,128,128]{3,2,1,0:T(8,128)} %get-tuple-element.11) | copy-start | bytes 1572868
  33.3 10.4 %copy-start.11 = (f32[1,8,128,128]{3,2,1,0:T(8,128)S(1)}, f32[1,8,128,128]{3,2,1,0:T(8,128)}, u32[]{:S(2)}) copy-start(f32[1,8,128,128]{3,2,1,0:T(8,128)} %get-tuple-element.5) | copy-start | bytes 1572868
  33.3 14.4 %collective-permute-start.1 = (f32[2,2,1,128,128]{4,3,1,2,0:T(8,128)S(1)}, f32[2,2,1,128,128]{4,3,1,2,0:T(8,128)S(1)}, u32[]{:S(2)}, u32[]{:S(2)}) collective-permute-start(f32[2,2,1,128,128]{4,3,1,2,0:T(8,128)S(1)} %pad_maximum_fusion.4), channel_id=1, source_target_pairs={{0,1},{1,2},{2,3},{3,4},{4,5},{5,6},{6,7},{8,9},{9,10},{10,11},{11... | collective-permute-start | bytes 786440 | tf_op jit(solution)/shard_map/ppermute | solution.py:34
  59.4 15.7 %copy-start.1 = (f32[2,8,128,128]{3,2,0,1:T(8,128)S(1)}, f32[2,8,128,128]{3,2,0,1:T(8,128)}, u32[]{:S(2)}) copy-start(f32[2,8,128,128]{3,2,0,1:T(8,128)} %copy-done) | copy-start | bytes 3145732
  59.4 15.7 %copy-start.10 = (f32[1,8,128,128]{3,2,1,0:T(8,128)S(1)}, f32[1,8,128,128]{3,2,1,0:T(8,128)}, u32[]{:S(2)}) copy-start(f32[1,8,128,128]{3,2,1,0:T(8,128)} %get-tuple-element.11) | copy-start | bytes 1572868
  59.4 15.7 %copy-start.12 = (f32[1,8,128,128]{3,2,1,0:T(8,128)S(1)}, f32[1,8,128,128]{3,2,1,0:T(8,128)}, u32[]{:S(2)}) copy-start(f32[1,8,128,128]{3,2,1,0:T(8,128)} %get-tuple-element.5) | copy-start | bytes 1572868
  59.4 15.7 %collective-permute-start.2 = (f32[2,2,1,128,128]{4,3,1,2,0:T(8,128)S(1)}, f32[2,2,1,128,128]{4,3,1,2,0:T(8,128)S(1)}, u32[]{:S(2)}, u32[]{:S(2)}) collective-permute-start(f32[2,2,1,128,128]{4,3,1,2,0:T(8,128)S(1)} %pad_maximum_fusion.5), channel_id=1, source_target_pairs={{1,0},{2,1},{3,2},{4,3},{5,4},{6,5},{7,6},{9,8},{10,9},{11,10},{12... | collective-permute-start | bytes 786440 | tf_op jit(solution)/shard_map/ppermute | solution.py:34
  76.7 8.1 %copy-start.25 = (f32[1,8,128,128]{3,2,1,0:T(8,128)S(1)}, f32[1,8,128,128]{3,2,1,0:T(8,128)}, u32[]{:S(2)}) copy-start(f32[1,8,128,128]{3,2,1,0:T(8,128)} %get-tuple-element.55) | copy-start | bytes 1572868
  76.8 8.0 %collective-permute-start.3 = (f32[2,2,1,128,128]{4,3,1,2,0:T(8,128)S(1)}, f32[2,2,1,128,128]{4,3,1,2,0:T(8,128)S(1)}, u32[]{:S(2)}, u32[]{:S(2)}) collective-permute-start(f32[2,2,1,128,128]{4,3,1,2,0:T(8,128)S(1)} %pad_maximum_fusion.6), channel_id=1, source_target_pairs={{0,1},{1,2},{2,3},{3,4},{4,5},{5,6},{6,7},{8,9},{9,10},{10,11},{11... | collective-permute-start | bytes 786440 | tf_op jit(solution)/shard_map/ppermute | solution.py:34
  86.3 13.1 %collective-permute-start.4 = (f32[2,2,1,128,128]{4,3,1,2,0:T(8,128)S(1)}, f32[2,2,1,128,128]{4,3,1,2,0:T(8,128)S(1)}, u32[]{:S(2)}, u32[]{:S(2)}) collective-permute-start(f32[2,2,1,128,128]{4,3,1,2,0:T(8,128)S(1)} %pad_maximum_fusion.7), channel_id=1, source_target_pairs={{1,0},{2,1},{3,2},{4,3},{5,4},{6,5},{7,6},{9,8},{10,9},{11,10},{12... | collective-permute-start | bytes 786440 | tf_op jit(solution)/shard_map/ppermute | solution.py:34
  100.9 7.3 %copy-start.24 = (f32[1,8,128,128]{3,2,1,0:T(8,128)S(1)}, f32[1,8,128,128]{3,2,1,0:T(8,128)}, u32[]{:S(2)}) copy-start(f32[1,8,128,128]{3,2,1,0:T(8,128)} %get-tuple-element.54) | copy-start | bytes 1572868
  100.9 7.2 %collective-permute-start.5 = (f32[2,2,1,128,128]{4,3,1,2,0:T(8,128)S(1)}, f32[2,2,1,128,128]{4,3,1,2,0:T(8,128)S(1)}, u32[]{:S(2)}, u32[]{:S(2)}) collective-permute-start(f32[2,2,1,128,128]{4,3,1,2,0:T(8,128)S(1)} %pad_maximum_fusion.8), channel_id=1, source_target_pairs={{0,1},{1,2},{2,3},{3,4},{4,5},{5,6},{6,7},{8,9},{9,10},{10,11},{11... | collective-permute-start | bytes 786440 | tf_op jit(solution)/shard_map/ppermute | solution.py:34
  109.7 13.1 %collective-permute-start.6 = (f32[2,2,1,128,128]{4,3,1,2,0:T(8,128)S(1)}, f32[2,2,1,128,128]{4,3,1,2,0:T(8,128)S(1)}, u32[]{:S(2)}, u32[]{:S(2)}) collective-permute-start(f32[2,2,1,128,128]{4,3,1,2,0:T(8,128)S(1)} %pad_maximum_fusion.9), channel_id=1, source_target_pairs={{1,0},{2,1},{3,2},{4,3},{5,4},{6,5},{7,6},{9,8},{10,9},{11,10},{12... | collective-permute-start | bytes 786440 | tf_op jit(solution)/shard_map/ppermute | solution.py:34
  124.2 7.2 %copy-start.7 = (f32[2,8,128,128]{3,2,1,0:T(8,128)}, f32[2,8,128,128]{3,2,1,0:T(8,128)S(1)}, u32[]{:S(2)}) copy-start(f32[2,8,128,128]{3,2,1,0:T(8,128)S(1)} %get-tuple-element.27) | copy-start | bytes 3145732
  124.3 7.1 %collective-permute-start.7 = (f32[2,2,1,128,128]{4,3,1,2,0:T(8,128)S(1)}, f32[2,2,1,128,128]{4,3,1,2,0:T(8,128)S(1)}, u32[]{:S(2)}, u32[]{:S(2)}) collective-permute-start(f32[2,2,1,128,128]{4,3,1,2,0:T(8,128)S(1)} %pad_maximum_fusion.10), channel_id=1, source_target_pairs={{0,1},{1,2},{2,3},{3,4},{4,5},{5,6},{6,7},{8,9},{9,10},{10,11},{11... | collective-permute-start | bytes 786440 | tf_op jit(solution)/shard_map/ppermute | solution.py:34
  127.1 4.3 %copy-start.23 = (f32[1,8,128,128]{3,2,1,0:T(8,128)S(1)}, f32[1,8,128,128]{3,2,1,0:T(8,128)}, u32[]{:S(2)}) copy-start(f32[1,8,128,128]{3,2,1,0:T(8,128)} %get-tuple-element.53) | copy-start | bytes 1572868
  139.8 39.2 %all-to-all-start.1 = ((f32[32,8,4,128]{3,2,1,0:T(4,128)}), f32[32,8,4,128]{3,2,1,0:T(4,128)}, u32[]{:S(2)}, u32[]{:S(2)}) async-start(f32[32,8,4,128]{3,2,1,0:T(4,128)} %gather_fusion), calls=%async_computation.1 | async-start | bytes 1048576 | tf_op jit(solution)/shard_map/all_to_all | solution.py:45
  162.5 4.5 %copy-start.8 = (f32[2,8,128,128]{3,2,1,0:T(8,128)S(1)}, f32[2,8,128,128]{3,2,1,0:T(8,128)}, u32[]{:S(2)}) copy-start(f32[2,8,128,128]{3,2,1,0:T(8,128)} %copy-done.7) | copy-start | bytes 3145732
  (22 other events, 44.3 us)
where the time goes:
time: 182 us; the launch traced here: 181 us
  waiting for transfers between devices  62.4 us (34%)
  starting transfers between devices  58.7 us (32%)
  local copies, waits for them, and re-layouts  30.4 us (17%)
  other arithmetic  26.6 us (15%)
  between operations  2.6 us (1%)
    ppermute x8, waiting for transfers between devices, from_behind(): return lax.ppermute(block, axis, route)  51.2 us
    ppermute x8, starting transfers between devices, from_behind(): return lax.ppermute(block, axis, route)  26.4 us
    all_to_all x1, starting transfers between devices, sum_at_owner(): lax.all_to_all(pieces, axis, split_axis=0, concat_axis=0, tiled=True)  22.7 us
    all_to_all x1, waiting for transfers between devices, sum_at_owner(): lax.all_to_all(pieces, axis, split_axis=0, concat_axis=0, tiled=True)  11.2 us
    all_to_all x1, starting transfers between devices, from_everyone(): return lax.all_to_all(copies, axis, split_axis=0, concat_axis=0, tiled=True)  9.53 us
    unnamed x78, local copies, waits for them, and re-layouts  9.21 us
    add x4, other arithmetic, per_device(): ez = ez + coef * (bwd_diff(hy, 2) - bwd_diff(hx, 3)) + drive  6.78 us
    another operation x4, local copies, waits for them, and re-layouts, per_device(): comps = [jnp.stack([fwd_fields[0, c], adj_fields[0, c]]) for c in range(6)]  5.93 us
  transfers between devices with their start and end apart: 10, of which 8 were waited for; matrix products, arithmetic and copies ran while one was open for 11% of the time, Pallas kernels for 0%

commit v1 on v0

v1 whole, which is shorter than its diff:
```python
import functools
import math

import jax
import jax.numpy as jnp
from jax import lax
from jax.experimental import pallas as pl
from jax.experimental.pallas import tpu as pltpu
from jax.sharding import PartitionSpec as P

STEPS = 4
COURANT = 0.5
AMPLITUDE = 4.0
MESH = pl.DeviceIdType.MESH
ROWS = 32
PAD = 8


def from_everyone(shard, axis):
    copies = jnp.broadcast_to(shard, (lax.axis_size(axis), *shard.shape))
    return lax.all_to_all(copies, axis, split_axis=0, concat_axis=0, tiled=True)


def sum_at_owner(shard, axis, dim):
    dims = shard.shape
    count = lax.axis_size(axis)
    pieces = shard.reshape(*dims[:dim], count, dims[dim] // count, *dims[dim + 1 :])
    pieces = jnp.moveaxis(pieces, dim, 0)
    arrived = lax.all_to_all(pieces, axis, split_axis=0, concat_axis=0, tiled=True)
    return arrived.sum(axis=0)


def filter_xy(values):
    padded = jnp.pad(values, ((0, 0), (1, 1), (1, 1)))
    rows = padded[:, :-2] + 2.0 * padded[:, 1:-1] + padded[:, 2:]
    return (rows[:, :, :-2] + 2.0 * rows[:, :, 1:-1] + rows[:, :, 2:]) / 16.0


def evolve_kernel(
    pos_ref, wave_ref, fwd_ref, adj_ref, coef_ref, out_ref, tot_ref,
    st, el, eu, ha, ha0, sup, sdn, drv, load_sem, store_sem, up_s, up_r, h_s, h_r, dn_s, dn_r,
):
    depth, width_x, width_y = coef_ref.shape
    top = depth - 1
    grp, slab = lax.axis_index("grp"), lax.axis_index("slab")
    slabs = lax.axis_size("slab")
    has_up, has_dn = slab < slabs - 1, slab > 0
    inner = pl.ds(PAD, width_x)
    fields = (fwd_ref, adj_ref)

    def up_copy(ev, n, src):
        return pltpu.make_async_remote_copy(
            src_ref=src, dst_ref=el.at[ev, n, :, pl.ds(0, width_x), :], send_sem=up_s.at[ev, n], recv_sem=up_r.at[ev, n],
            device_id=(grp, slab + 1), device_id_type=MESH)

    def h_copy(ev):
        return pltpu.make_async_remote_copy(
            src_ref=fields[ev].at[0, 3:5, top], dst_ref=ha0.at[ev], send_sem=h_s.at[ev], recv_sem=h_r.at[ev],
            device_id=(grp, slab + 1), device_id_type=MESH)

    def dn_copy(ev, n, src):
        return pltpu.make_async_remote_copy(
            src_ref=src, dst_ref=eu.at[ev, n], send_sem=dn_s.at[ev, n], recv_sem=dn_r.at[ev, n],
            device_id=(grp, slab - 1), device_id_type=MESH)

    barrier = pltpu.get_barrier_semaphore()

    @pl.when(has_up)
    def _():
        pl.semaphore_signal(barrier, inc=1, device_id=(grp, slab + 1), device_id_type=MESH)

    @pl.when(has_dn)
    def _():
        pl.semaphore_signal(barrier, inc=1, device_id=(grp, slab - 1), device_id_type=MESH)

    loads = [
        pltpu.make_async_copy(fields[ev].at[0], st.at[ev, :, :, inner, :], load_sem.at[ev]) for ev in range(2)
    ]
    for copy in loads:
        copy.start()

    zeros = jnp.zeros((PAD, width_y), jnp.float32)

    @pl.loop(0, depth)
    def _(z):
        for ev in range(2):
            for c in (1, 2):
                st[ev, c, z, PAD + width_x :, :] = zeros
            for c in (4, 5):
                st[ev, c, z, :PAD, :] = zeros

    for ev in range(2):
        for n in range(STEPS):
            el[ev, n, 2, width_x:, :] = zeros
    row = lax.broadcasted_iota(jnp.int32, (width_x, width_y), 0)
    col = lax.broadcasted_iota(jnp.int32, (width_x, width_y), 1)
    dx = (row - pos_ref[0, 1]).astype(jnp.float32) / (width_x / 4.0)
    dy = (col - pos_ref[0, 2]).astype(jnp.float32) / (width_y / 4.0)
    profile = jnp.exp(-0.5 * (dx * dx + dy * dy))
    wave = jnp.full((8, width_y), wave_ref[0], jnp.int32).astype(jnp.float32)
    omega = 2.0 * math.pi / (6.0 + 2.0 * wave)
    for n in range(STEPS):
        drv[n] = (AMPLITUDE * jnp.sin(omega * (n + 1.0)))[:1] * profile
    lane = lax.broadcasted_iota(jnp.int32, (ROWS, width_y), 1)
    is_first, is_last = lane == 0, lane == width_y - 1

    @pl.when(jnp.logical_not(has_up))
    def _():
        eu[...] = jnp.zeros_like(eu)

    @pl.when(jnp.logical_not(has_dn))
    def _():
        ha[...] = jnp.zeros_like(ha)

    pl.semaphore_wait(barrier, has_up.astype(jnp.int32) + has_dn.astype(jnp.int32))
    for ev in range(2):

        @pl.when(has_up)
        def _():
            up_copy(ev, 0, fields[ev].at[0, 0:3, top]).start()
            h_copy(ev).start()

        @pl.when(has_dn)
        def _():
            dn_copy(ev, 0, fields[ev].at[0, 0:2, 0]).start()

    def next_y(v):
        return jnp.where(is_last, 0.0, pltpu.roll(v, width_y - 1, axis=1))

    def prev_y(v):
        return jnp.where(is_first, 0.0, pltpu.roll(v, 1, axis=1))

    def chunks():
        return [(r, pl.ds(PAD + r, ROWS)) for r in range(0, width_x, ROWS)]

    def h_layer(ev, z, above):
        for r, here in chunks():
            ahead = pl.ds(PAD + r + 1, ROWS)
            ex, ey, ez = (st[ev, c, z, here, :] for c in range(3))
            exu, eyu = above(r)
            dyz = next_y(ez) - ez
            dyx = next_y(ex) - ex
            st[ev, 3, z, here, :] += -COURANT * (dyz - (eyu - ey))
            st[ev, 4, z, here, :] += -COURANT * ((exu - ex) - (st[ev, 2, z, ahead, :] - ez))
            st[ev, 5, z, here, :] += -COURANT * ((st[ev, 1, z, ahead, :] - ey) - dyx)

    def e_layer(ev, n, z, below, send=None):
        plane = jnp.where((slab * depth + z == pos_ref[0, 0]) & (ev == 0), 1.0, 0.0)
        for r, here in chunks():
            back = pl.ds(PAD + r - 1, ROWS)
            out = pl.ds(r, ROWS)
            hx, hy, hz = (st[ev, c, z, here, :] for c in range(3, 6))
            hxd, hyd = below(r)
            coef = coef_ref[z, out, :]
            ex = st[ev, 0, z, here, :] + coef * ((hz - prev_y(hz)) - (hy - hyd))
            ey = st[ev, 1, z, here, :] + coef * ((hx - hxd) - (hz - st[ev, 5, z, back, :]))
            ez = st[ev, 2, z, here, :] + coef * ((hy - st[ev, 4, z, back, :]) - (hx - prev_y(hx)))
            ez = ez + plane * drv[n, out, :]
            for c, v in enumerate((ex, ey, ez)):
                st[ev, c, z, here, :] = v
            if send is not None:
                for c in range(send.shape[0]):
                    send[c, out, :] = (ex, ey, ez)[c]

    @pl.loop(0, 2 * STEPS)
    def _(i):
        n, ev = i // 2, lax.rem(i, 2)

        @pl.when(n == 0)
        def _():
            pltpu.make_async_copy(fwd_ref.at[0], st.at[ev, :, :, inner, :], load_sem.at[ev]).wait()

        @pl.loop(0, top)
        def _(z):
            h_layer(ev, z, lambda r: (st[ev, 0, z + 1, pl.ds(PAD + r, ROWS), :], st[ev, 1, z + 1, pl.ds(PAD + r, ROWS), :]))

        def below(z):
            return lambda r: (st[ev, 3, z - 1, pl.ds(PAD + r, ROWS), :], st[ev, 4, z - 1, pl.ds(PAD + r, ROWS), :])

        @pl.loop(1, top)
        def _(z):
            e_layer(ev, n, z, below(z))

        @pl.when(has_up)
        def _():
            dn_copy(ev, n, sdn.at[ev, n]).wait_recv()

        h_layer(ev, top, lambda r: (eu[ev, n, 0, pl.ds(r, ROWS), :], eu[ev, n, 1, pl.ds(r, ROWS), :]))
        e_layer(ev, n, top, below(top), sup.at[ev, n])

        @pl.when(has_up & (n < STEPS - 1))
        def _():
            up_copy(ev, n + 1, sup.at[ev, n]).start()

        @pl.when(has_dn)
        def _():
            up_copy(ev, n, sup.at[ev, n]).wait_recv()

            @pl.when(n == 0)
            def _():
                pltpu.make_async_remote_copy(
                    src_ref=fwd_ref.at[0, 3:5, top], dst_ref=ha0.at[ev], send_sem=h_s.at[ev], recv_sem=h_r.at[ev],
                    device_id=(grp, slab - 1), device_id_type=MESH).wait_recv()
                ha[ev] = ha0[ev]

            for r, here in chunks():
                out, ahead = pl.ds(r, ROWS), pl.ds(r + 1, ROWS)
                ex, ey, ez = (el[ev, n, c, out, :] for c in range(3))
                ha[ev, 0, out, :] += -COURANT * ((next_y(ez) - ez) - (st[ev, 1, 0, here, :] - ey))
                ha[ev, 1, out, :] += -COURANT * ((st[ev, 0, 0, here, :] - ex) - (el[ev, n, 2, ahead, :] - ez))

        e_layer(ev, n, 0, lambda r: (ha[ev, 0, pl.ds(r, ROWS), :], ha[ev, 1, pl.ds(r, ROWS), :]), sdn.at[ev, n])

        @pl.when(has_dn & (n < STEPS - 1))
        def _():
            dn_copy(ev, n + 1, sdn.at[ev, n]).start()

        @pl.when(i == 2 * STEPS - 2)
        def _():
            pltpu.make_async_copy(st.at[0, :, :, inner, :], out_ref.at[0], store_sem).start()

        @pl.when(ev == 1)
        def _():
            @pl.loop(0, depth)
            def _(z):
                for r, here in chunks():
                    out = pl.ds(r, ROWS)
                    new = sum(st[0, c, z, here, :] * st[1, c, z, here, :] for c in range(3))
                    old = jnp.where(n == 0, 0.0, tot_ref[z, out, :])
                    tot_ref[z, out, :] = old + new

    pltpu.make_async_copy(st.at[0, :, :, inner, :], out_ref.at[0], store_sem).wait()
    for ev in range(2):

        @pl.when(has_up)
        def _():
            up_copy(ev, 0, fields[ev].at[0, 0:3, top]).wait_send()
            h_copy(ev).wait_send()
            for n in range(1, STEPS):
                up_copy(ev, n, sup.at[ev, n - 1]).wait_send()

        @pl.when(has_dn)
        def _():
            dn_copy(ev, 0, fields[ev].at[0, 0:2, 0]).wait_send()
            for n in range(1, STEPS):
                dn_copy(ev, n, sdn.at[ev, n - 1]).wait_send()


def evolve(fwd_fields, adj_fields, coef, source_pos, wave_idx):
    depth, width_x, width_y = coef.shape
    f32 = jnp.float32
    layer = (width_x, width_y)
    smem = pl.BlockSpec(memory_space=pltpu.SMEM)
    vmem = pl.BlockSpec(memory_space=pltpu.VMEM)
    hbm = pl.BlockSpec(memory_space=pl.ANY)
    dma = pltpu.SemaphoreType.DMA
    return pl.pallas_call(
        evolve_kernel,
        out_shape=(
            jax.ShapeDtypeStruct(fwd_fields.shape, f32),
            jax.ShapeDtypeStruct(coef.shape, f32),
        ),
        in_specs=[smem, smem, hbm, hbm, vmem],
        out_specs=(hbm, vmem),
        scratch_shapes=[
            pltpu.VMEM((2, 6, depth, width_x + 2 * PAD, width_y), f32),
            pltpu.VMEM((2, STEPS, 3, width_x + PAD, width_y), f32),
            pltpu.VMEM((2, STEPS, 2, *layer), f32),
            pltpu.VMEM((2, 2, *layer), f32),
            pltpu.VMEM((2, 2, *layer), f32),
            pltpu.VMEM((2, STEPS, 3, *layer), f32),
            pltpu.VMEM((2, STEPS, 2, *layer), f32),
            pltpu.VMEM((STEPS, *layer), f32),
            dma((2,)), dma(()), dma((2, STEPS)), dma((2, STEPS)), dma((2,)), dma((2,)), dma((2, STEPS)), dma((2, STEPS)),
        ],
        compiler_params=pltpu.CompilerParams(collective_id=0, has_side_effects=True, vmem_limit_bytes=40 << 20),
        name="evolve",
    )(source_pos, wave_idx, fwd_fields, adj_fields, coef)


def per_device(
    fwd_fields, adj_fields, density, block_ids, material_idx, material_eps, source_pos, wave_idx
):
    depth, width_x, width_y = fwd_fields.shape[2:]
    nblock = block_ids.shape[0]
    block_rows = width_x // nblock
    pieces = from_everyone(density, "grp")
    blocks = jnp.moveaxis(pieces, 0, 1)
    placed = jnp.zeros_like(blocks).at[:, block_ids].set(blocks).reshape(depth, width_x, width_y)
    smooth = filter_xy(placed)
    onehot = (
        material_idx[:, None] == jnp.arange(material_eps.shape[0], dtype=jnp.int32)[None, :]
    ).astype(jnp.float32)
    base = jnp.sum(onehot * material_eps[None, :], axis=1)
    base_rows = jnp.repeat(base, block_rows)
    eps = base_rows[None, :, None] + 3.0 * smooth
    coef = 0.5 / eps
    finals, total = evolve(fwd_fields, adj_fields, coef, source_pos, wave_idx)
    grad_sum = sum_at_owner(
        filter_xy(total)
        .reshape(depth, nblock, block_rows, width_y)[:, block_ids]
        .reshape(depth, width_x, width_y),
        "grp",
        1,
    )
    scale = 3.0 / (STEPS * math.sqrt(lax.axis_size("grp")))
    return (finals, grad_sum * scale)


def solution(mesh):
    placed = (
        P("grp", None, "slab", None, None),
        P("grp", None, "slab", None, None),
        P("slab", "grp", None),
        P(),
        P(),
        P(),
        P("grp", None),
        P("grp"),
    )
    return jax.shard_map(
        per_device,
        mesh=mesh,
        in_specs=placed,
        out_specs=(P("grp", None, "slab", None, None), P("slab", "grp", None)),
        check_vma=False,
    )
```

time: 182 us -> 157 us (0.86)
  Pallas kernels: 0 us -> 46.9 us
  waiting for transfers between devices: 62.4 us -> 30.6 us
  other arithmetic: 26.6 us -> 6.41 us
  local copies, waits for them, and re-layouts: 30.4 us -> 15.8 us
  starting transfers between devices: 58.7 us -> 55.4 us
    ppermute x8 -> x0, waiting for transfers between devices: 51.2 us -> none  [from_behind(): return lax.ppermute(block, axis, route)]
    pallas_call x0 -> x1, Pallas kernels: none -> 46.9 us  [evolve(): pl.pallas_call(evolve_kernel, out_shape=(jax.ShapeDtypeStruct(fwd_fields....]
    ppermute x8 -> x0, starting transfers between devices: 26.4 us -> none  [from_behind(): return lax.ppermute(block, axis, route)]
    all_to_all x1, starting transfers between devices: 22.7 us -> 46.2 us  [sum_at_owner(): lax.all_to_all(pieces, axis, split_axis=0, concat_axis=0, tiled=True)]
    all_to_all x1, waiting for transfers between devices: 0.01 us -> 14.2 us  [from_everyone(): return lax.all_to_all(copies, axis, split_axis=0, concat_axis=0, tiled=True)]
    add x5 -> x0, other arithmetic: 8.18 us -> none  [the longest x4 6.78 us: per_device(): ez = ez + coef * (bwd_diff(hy, 2) - bwd_diff(hx, 3)) + drive]
    another operation x19 -> x0, local copies, waits for them, and re-layouts: 6.91 us -> none  [the longest x4 5.93 us: per_device(): comps = [jnp.stack([fwd_fields[0, c], adj_fields[0, c]]) for c in range(6)]]
    sub x5 -> x0, other arithmetic: 6.05 us -> none  [the longest x4 4.96 us: per_device(): hx = hx - COURANT * (fwd_diff(ez, 3) - above_diff(ey, upper[1]))]
  transfers between devices with their start and end apart: 10 -> 2, of which waited for: 8 -> 2; matrix products, arithmetic and copies ran while one was open for 11% -> 1% of each run, Pallas kernels for 0% -> 0%
where the time goes in v1:
time: 157 us
  starting transfers between devices  55.4 us (35%)
  Pallas kernels  46.9 us (30%)
  waiting for transfers between devices  30.6 us (19%)
  local copies, waits for them, and re-layouts  15.8 us (10%)
  other arithmetic  6.41 us (4%)
    pallas_call x1, Pallas kernels, evolve(): pl.pallas_call(evolve_kernel, out_shape=(jax.ShapeDtypeStruct(fwd_fields....  46.9 us
    all_to_all x1, starting transfers between devices, sum_at_owner(): lax.all_to_all(pieces, axis, split_axis=0, concat_axis=0, tiled=True)  46.2 us
    all_to_all x1, waiting for transfers between devices, sum_at_owner(): lax.all_to_all(pieces, axis, split_axis=0, concat_axis=0, tiled=True)  16.5 us
    all_to_all x1, waiting for transfers between devices, from_everyone(): return lax.all_to_all(copies, axis, split_axis=0, concat_axis=0, tiled=True)  14.2 us
    all_to_all x1, starting transfers between devices, from_everyone(): return lax.all_to_all(copies, axis, split_axis=0, concat_axis=0, tiled=True)  9.19 us
    scatter x2, local copies, waits for them, and re-layouts, per_device(): jnp.zeros_like(blocks).at[:, block_ids].set(blocks)  6.37 us
    unnamed x14, local copies, waits for them, and re-layouts  4.85 us
  transfers between devices with their start and end apart: 2, of which 2 were waited for; matrix products, arithmetic and copies ran while one was open for 1% of the time, Pallas kernels for 0%

profile of v1, /device:TPU:25, one launch (start us, length us, event | category | flops | bytes accessed | tf_op | source)
XLA Modules:
  0.0 156.6 jit_solution(13604095718274278147)
XLA Ops:
  0.6 0.7 copy.14
  1.3 0.9 broadcast_in_dim.19
  2.2 9.2 %all-to-all-start = ((f32[32,8,4,128]{3,1,2,0:T(8,128)}), f32[32,8,4,128]{3,1,2,0:T(8,128)S(1)}, u32[]{:S(2)}, u32[]{:S(2)}) async-start(f32[32,8,4,128]{3,1,2,0:T(8,128)} %broadcast_in_dim.19), calls=%async_computation | async-start | bytes 1048576 | tf_op jit(solution)/shard_map/all_to_all | solution.py:21
  11.4 0.8 select_reduce_fusion
  12.2 0.1 broadcast_in_dim.16
  12.2 0.1 add.42
  13.0 0.7 compare_select_fusion
  13.7 14.2 %all-to-all-done = f32[32,8,4,128]{3,1,2,0:T(8,128)S(1)} async-done(((f32[32,8,4,128]{3,1,2,0:T(8,128)}), f32[32,8,4,128]{3,1,2,0:T(8,128)S(1)}, u32[]{:S(2)}, u32[]{:S(2)}) %all-to-all-start) | async-done | bytes 524320 | tf_op jit(solution)/shard_map/all_to_all | solution.py:21
  27.8 0.8 copy-done.5
  28.6 0.9 broadcast_in_dim.17
  29.5 5.0 %scatter_fusion = f32[8,32,4,128]{3,0,2,1:T(8,128)} fusion(f32[8,32,4,128]{3,0,2,1:T(8,128)} %broadcast_in_dim.17, s32[32]{0:T(128)S(1)} %compare_select_fusion, f32[32,8,4,128]{3,1,2,0:T(8,128)} %copy-done.5), kind=kCustom, calls=%fused_computation.1 | custom fusion | bytes 1572992 | tf_op jit(solution)/shard_map/scatter | solution.py:289
  34.5 1.3 copy.15
  35.9 0.9 fusion.1
  36.7 0.4 fusion.10.coef_ref
  37.2 46.9 %evolve.1 = (f32[1,6,8,128,128]{4,3,2,1,0:T(8,128)S(1)}, f32[8,128,128]{2,1,0:T(8,128)S(1)}) custom-call(s32[1,3]{1,0:T(1,128)S(1)} %copy-done.4, s32[1]{0:T(128)S(6)} %copy.18.wave_ref, f32[1,6,8,128,128]{4,3,2,1,0:T(8,128)S(1)} %copy-done, f32[1,6,8,128,128]{4,3,2,1,0:T(8,128)S(1)} %copy-done.1, f32[8,128,128]{2,1,0:T(8,128)S(1)} %fusion.10.coef_ref), custom_call_target="tpu_custom_call" | custom-call | tf_op jit(solution)/shard_map/evolve/pallas_call | solution.py:257
  84.0 1.7 %copy-done.2 = f32[1,6,8,128,128]{4,3,2,1,0:T(8,128)} copy-done((f32[1,6,8,128,128]{4,3,2,1,0:T(8,128)}, f32[1,6,8,128,128]{4,3,2,1,0:T(8,128)S(1)}, u32[]{:S(2)}) %copy-start.2) | copy-done | bytes 3145752
  85.7 0.9 fusion.4
  86.6 1.1 fusion.6
  87.7 2.7 %gather_fusion = f32[32,8,4,128]{3,2,1,0:T(4,128)} fusion(f32[8,32,4,128]{3,2,1,0:T(4,128)} %bitcast.3, s32[1024]{0:T(1024)S(1)} %pad_clamp_fusion), kind=kCustom, calls=%fused_computation | custom fusion | bytes 1048704 | tf_op jit(solution)/shard_map/gather | solution.py:300
  90.4 46.2 %all-to-all-start.1 = ((f32[32,8,4,128]{3,2,1,0:T(4,128)}), f32[32,8,4,128]{3,2,1,0:T(4,128)}, u32[]{:S(2)}, u32[]{:S(2)}) async-start(f32[32,8,4,128]{3,2,1,0:T(4,128)} %gather_fusion), calls=%async_computation.1 | async-start | bytes 1048576 | tf_op jit(solution)/shard_map/all_to_all | solution.py:29
  136.7 16.5 %all-to-all-done.1 = f32[32,8,4,128]{3,2,1,0:T(4,128)} async-done(((f32[32,8,4,128]{3,2,1,0:T(4,128)}), f32[32,8,4,128]{3,2,1,0:T(4,128)}, u32[]{:S(2)}, u32[]{:S(2)}) %all-to-all-start.1) | async-done | bytes 524320 | tf_op jit(solution)/shard_map/all_to_all | solution.py:29
  153.2 1.1 reduce_sum.19
  154.3 0.6 broadcast_multiply_fusion
  154.9 1.7 %copy.19 = f32[1,6,8,128,128]{4,3,2,1,0:T(8,128)} copy(f32[1,6,8,128,128]{4,3,2,1,0:T(8,128)S(1)} %copy-done.3) | data formatting | bytes 6291456
  (11 shorter events, 0.0 us)
Async XLA Ops:
  2.2 25.6 %all-to-all-start = ((f32[32,8,4,128]{3,1,2,0:T(8,128)}), f32[32,8,4,128]{3,1,2,0:T(8,128)S(1)}, u32[]{:S(2)}, u32[]{:S(2)}) async-start(f32[32,8,4,128]{3,1,2,0:T(8,128)} %broadcast_in_dim.19), calls=%async_computation | async-start | bytes 1048576 | tf_op jit(solution)/shard_map/all_to_all | solution.py:21
  27.8 0.8 copy-start.5
  29.5 7.6 %copy-start = (f32[1,6,8,128,128]{4,3,2,1,0:T(8,128)S(1)}, f32[1,6,8,128,128]{4,3,2,1,0:T(8,128)}, u32[]{:S(2)}) copy-start(f32[1,6,8,128,128]{4,3,2,1,0:T(8,128)} %fwd_ref.1) | copy-start | bytes 9437188
  29.5 7.7 %copy-start.4 = (s32[1,3]{1,0:T(1,128)S(1)}, s32[1,3]{1,0:T(1,128)}, u32[]{:S(2)}) copy-start(s32[1,3]{1,0:T(1,128)} %pos_ref.1) | copy-start | bytes 40
  34.5 2.6 %copy-start.1 = (f32[1,6,8,128,128]{4,3,2,1,0:T(8,128)S(1)}, f32[1,6,8,128,128]{4,3,2,1,0:T(8,128)}, u32[]{:S(2)}) copy-start(f32[1,6,8,128,128]{4,3,2,1,0:T(8,128)} %adj_ref.1) | copy-start | bytes 9437188
  84.0 1.7 %copy-start.2 = (f32[1,6,8,128,128]{4,3,2,1,0:T(8,128)}, f32[1,6,8,128,128]{4,3,2,1,0:T(8,128)S(1)}, u32[]{:S(2)}) copy-start(f32[1,6,8,128,128]{4,3,2,1,0:T(8,128)S(1)} %get-tuple-element.8) | copy-start | bytes 9437188
  85.7 69.2 %copy-start.3 = (f32[1,6,8,128,128]{4,3,2,1,0:T(8,128)S(1)}, f32[1,6,8,128,128]{4,3,2,1,0:T(8,128)}, u32[]{:S(2)}) copy-start(f32[1,6,8,128,128]{4,3,2,1,0:T(8,128)} %copy-done.2) | copy-start | bytes 9437188
  90.4 62.7 %all-to-all-start.1 = ((f32[32,8,4,128]{3,2,1,0:T(4,128)}), f32[32,8,4,128]{3,2,1,0:T(4,128)}, u32[]{:S(2)}, u32[]{:S(2)}) async-start(f32[32,8,4,128]{3,2,1,0:T(4,128)} %gather_fusion), calls=%async_computation.1 | async-start | bytes 1048576 | tf_op jit(solution)/shard_map/all_to_all | solution.py:29

commit v2 on v1

v2 whole, which is shorter than its diff:
```python
import math

import jax
import jax.numpy as jnp
from jax import lax
from jax.experimental import pallas as pl
from jax.experimental.pallas import tpu as pltpu
from jax.sharding import PartitionSpec as P

STEPS = 4
COURANT = 0.5
AMPLITUDE = 4.0
MESH = pl.DeviceIdType.MESH
ROWS = 32
PAD = 8
GROUPS = 32
RUNS = 4
OWN = 32
INNER = 24
HIGHEST = lax.Precision.HIGHEST


def evolve_kernel(
    pos_ref, wave_ref, ids_ref, mat_ref, eps_ref, dens_ref, fwd_ref, adj_ref, out_ref, grad_ref,
    st, coef_ref, tot_ref, el, eu, ha, ha0, sup, sdn, drv, rel, relh, gath, sendb, recvb, wmat, wtr, base,
    load_sem, store_sem, u1_s, u1_r, u2_s, u2_r, h1_s, h1_r, h2_s, h2_r, d1_s, d1_r, d2_s, d2_r,
    rl_s, rl_r, rh_s, rh_r, ga_s, ga_r, ri_s, ri_r, rb_s, rb_r,
):
    depth, width_x, width_y = coef_ref.shape
    top = depth - 1
    grp, slab = lax.axis_index("grp"), lax.axis_index("slab")
    slabs = lax.axis_size("slab")
    last = slabs - 1
    low, high = slabs // 2 - 1, slabs // 2
    has_up, has_dn = slab < last, slab > 0
    run = grp // (GROUPS // RUNS)
    mid = (run == 1) | (run == 2)
    mid_low, mid_high = mid & (slab == low), mid & (slab == high)
    relay_up, relay_dn = mid & (slab == 0), mid & (slab == last)
    inner = pl.ds(PAD, width_x)
    whole = pl.ds(0, width_x)
    fields = (fwd_ref, adj_ref)

    def copy_to(src, dst, send, recv, to_slab):
        return pltpu.make_async_remote_copy(
            src_ref=src, dst_ref=dst, send_sem=send, recv_sem=recv, device_id=(grp, to_slab), device_id_type=MESH)

    def u1(ev, n, src):
        return copy_to(src, el.at[ev, n, 0:2, whole, :], u1_s.at[ev, n], u1_r.at[ev, n], slab + 1)

    def u2(ev, n, src):
        return copy_to(src, el.at[ev, n, 2, whole, :], u2_s.at[ev, n], u2_r.at[ev, n], slab + 1)

    def u2_via(ev, n, src):
        return copy_to(src, rel.at[ev, n], u2_s.at[ev, n], rl_r.at[ev, n], 0)

    def h1(ev, src):
        return copy_to(src, ha0.at[ev, 1], h1_s.at[ev], h1_r.at[ev], slab + 1)

    def h2(ev, src):
        return copy_to(src, ha0.at[ev, 0], h2_s.at[ev], h2_r.at[ev], slab + 1)

    def h2_via(ev, src):
        return copy_to(src, relh.at[ev], h2_s.at[ev], rh_r.at[ev], 0)

    def d1(ev, n, src):
        return copy_to(src, eu.at[ev, n, 0], d1_s.at[ev, n], d1_r.at[ev, n], slab - 1)

    def d2(ev, n, src):
        return copy_to(src, eu.at[ev, n, 1], d2_s.at[ev, n], d2_r.at[ev, n], slab - 1)

    def d2_via(ev, n, src):
        return copy_to(src, rel.at[ev, n], d2_s.at[ev, n], rl_r.at[ev, n], last)

    def relay_e_up(ev, n):
        return copy_to(rel.at[ev, n], el.at[ev, n, 2, whole, :], rl_s.at[ev, n], u2_r.at[ev, n], high)

    def relay_h_up(ev):
        return copy_to(relh.at[ev], ha0.at[ev, 0], rh_s.at[ev], h2_r.at[ev], high)

    def relay_e_dn(ev, n):
        return copy_to(rel.at[ev, n], eu.at[ev, n, 1], rl_s.at[ev, n], d2_r.at[ev, n], low)

    def peer_copy(src, dst, send, recv, peer):
        return pltpu.make_async_remote_copy(
            src_ref=src, dst_ref=dst, send_sem=send, recv_sem=recv, device_id=(peer, slab), device_id_type=MESH)

    def peer_of(d):
        return lax.rem(grp + d, GROUPS)

    def own_rows(k, first, count):
        return pl.ds(pl.multiple_of(k * OWN + first, 8), count)

    def gather_copy(d):
        return peer_copy(dens_ref, gath.at[own_rows(grp, 0, OWN), :], ga_s.at[d], ga_r.at[grp], peer_of(d))

    def sums_copy(d, first, count, send, recv):
        return peer_copy(sendb.at[own_rows(peer_of(d), first, count), :], recvb.at[own_rows(grp, first, count), :],
                         send.at[d], recv.at[grp], peer_of(d))

    barrier = pltpu.get_barrier_semaphore()

    @pl.loop(1, GROUPS)
    def _(d):
        pl.semaphore_signal(barrier, inc=1, device_id=(peer_of(d), slab), device_id_type=MESH)

    def greet(cond, to_slab):
        @pl.when(cond)
        def _():
            pl.semaphore_signal(barrier, inc=1, device_id=(grp, to_slab), device_id_type=MESH)

    greet(has_up, slab + 1)
    greet(has_dn, slab - 1)
    greet(mid_low | mid_high, 0)
    greet(mid_low | mid_high, last)
    greet(relay_up | relay_dn, low)
    greet(relay_up | relay_dn, high)

    for ev in range(2):
        pltpu.make_async_copy(fields[ev].at[0], st.at[ev, :, :, inner, :], load_sem.at[ev]).start()

    zeros = jnp.zeros((PAD, width_y), jnp.float32)

    @pl.loop(0, depth)
    def _(z):
        for ev in range(2):
            for c in (1, 2):
                st[ev, c, z, PAD + width_x :, :] = zeros
            for c in (4, 5):
                st[ev, c, z, :PAD, :] = zeros

    for ev in range(2):
        for n in range(STEPS):
            el[ev, n, 2, width_x:, :] = zeros
    row = lax.broadcasted_iota(jnp.int32, (width_x, width_y), 0)
    col = lax.broadcasted_iota(jnp.int32, (width_x, width_y), 1)
    dx = (row - pos_ref[0, 1]).astype(jnp.float32) / (width_x / 4.0)
    dy = (col - pos_ref[0, 2]).astype(jnp.float32) / (width_y / 4.0)
    profile = jnp.exp(-0.5 * (dx * dx + dy * dy))
    wave = jnp.full((8, width_y), wave_ref[0], jnp.int32).astype(jnp.float32)
    omega = 2.0 * math.pi / (6.0 + 2.0 * wave)
    for n in range(STEPS):
        drv[n] = (AMPLITUDE * jnp.sin(omega * (n + 1.0)))[:1] * profile

    blocks = ids_ref.shape[0]
    block_rows = width_x // blocks
    slot = lax.rem(col, blocks)
    target = col // blocks
    for k in range(blocks):
        target = target + jnp.where(slot == k, ids_ref[k] * block_rows, 0)
    apart = jnp.abs(row - target)
    weights = jnp.where(apart == 0, 0.5, jnp.where(apart == 1, 0.25, 0.0))
    wmat[...] = weights
    wtr[...] = weights.T
    part = lax.broadcasted_iota(jnp.int32, (8, width_y), 0) // block_rows
    per_tile = 8 // block_rows
    for tile in range(width_x // 8):
        value = jnp.zeros((8, width_y), jnp.float32)
        for q in range(per_tile):
            value = jnp.where(part == q, eps_ref[mat_ref[tile * per_tile + q]], value)
        base[8 * tile : 8 * tile + 8, :] = value
    lane = lax.broadcasted_iota(jnp.int32, (ROWS, width_y), 1)
    is_first, is_last = lane == 0, lane == width_y - 1

    @pl.when(jnp.logical_not(has_up))
    def _():
        eu[...] = jnp.zeros_like(eu)

    @pl.when(jnp.logical_not(has_dn))
    def _():
        ha[...] = jnp.zeros_like(ha)

    own = pl.ds(pl.multiple_of(grp * OWN, 8), OWN)
    gath[own, :] = dens_ref[...]
    extra = jnp.where(mid_low | mid_high | relay_up | relay_dn, 2, 0)
    pl.semaphore_wait(barrier, GROUPS - 1 + has_up.astype(jnp.int32) + has_dn.astype(jnp.int32) + extra)

    def send_first(ev):
        f = fields[ev]

        @pl.when(has_dn)
        def _():
            d1(ev, 0, f.at[0, 0, 0]).start()

            @pl.when(mid_high)
            def _():
                d2_via(ev, 0, f.at[0, 1, 0]).start()

            @pl.when(jnp.logical_not(mid_high))
            def _():
                d2(ev, 0, f.at[0, 1, 0]).start()

        @pl.when(has_up)
        def _():
            @pl.when(mid_low)
            def _():
                u2_via(ev, 0, f.at[0, 2, top]).start()
                h2_via(ev, f.at[0, 3, top]).start()

            @pl.when(jnp.logical_not(mid_low))
            def _():
                u2(ev, 0, f.at[0, 2, top]).start()
                h2(ev, f.at[0, 3, top]).start()

            u1(ev, 0, f.at[0, 0:2, top]).start()
            h1(ev, f.at[0, 4, top]).start()

    send_first(0)

    @pl.loop(1, GROUPS)
    def _(d):
        gather_copy(d).start()

    send_first(1)

    def next_y(v):
        return jnp.where(is_last, 0.0, pltpu.roll(v, width_y - 1, axis=1))

    def prev_y(v):
        return jnp.where(is_first, 0.0, pltpu.roll(v, 1, axis=1))

    def chunks():
        return [(r, pl.ds(PAD + r, ROWS)) for r in range(0, width_x, ROWS)]

    def h_layer(ev, z, above):
        for r, here in chunks():
            ahead = pl.ds(PAD + r + 1, ROWS)
            ex, ey, ez = (st[ev, c, z, here, :] for c in range(3))
            exu, eyu = above(r)
            dyz = next_y(ez) - ez
            dyx = next_y(ex) - ex
            st[ev, 3, z, here, :] += -COURANT * (dyz - (eyu - ey))
            st[ev, 4, z, here, :] += -COURANT * ((exu - ex) - (st[ev, 2, z, ahead, :] - ez))
            st[ev, 5, z, here, :] += -COURANT * ((st[ev, 1, z, ahead, :] - ey) - dyx)

    def e_layer(ev, n, z, below, send=None):
        plane = jnp.where((slab * depth + z == pos_ref[0, 0]) & (ev == 0), 1.0, 0.0)
        for r, here in chunks():
            back = pl.ds(PAD + r - 1, ROWS)
            out = pl.ds(r, ROWS)
            hx, hy, hz = (st[ev, c, z, here, :] for c in range(3, 6))
            hxd, hyd = below(r)
            coef = coef_ref[z, out, :]
            ex = st[ev, 0, z, here, :] + coef * ((hz - prev_y(hz)) - (hy - hyd))
            ey = st[ev, 1, z, here, :] + coef * ((hx - hxd) - (hz - st[ev, 5, z, back, :]))
            ez = st[ev, 2, z, here, :] + coef * ((hy - st[ev, 4, z, back, :]) - (hx - prev_y(hx)))
            ez = ez + plane * drv[n, out, :]
            for c, v in enumerate((ex, ey, ez)):
                st[ev, c, z, here, :] = v
            if send is not None:
                for c in range(send.shape[0]):
                    send[c, out, :] = (ex, ey, ez)[c]

    def filter_y(v):
        left = jnp.where(col == 0, 0.0, pltpu.roll(v, 1, axis=1))
        right = jnp.where(col == width_y - 1, 0.0, pltpu.roll(v, width_y - 1, axis=1))
        return (left + 2.0 * v + right) * 0.25

    def h_inside(ev, z):
        h_layer(ev, z, lambda r: (st[ev, 0, z + 1, pl.ds(PAD + r, ROWS), :], st[ev, 1, z + 1, pl.ds(PAD + r, ROWS), :]))

    def below(ev, z):
        return lambda r: (st[ev, 3, z - 1, pl.ds(PAD + r, ROWS), :], st[ev, 4, z - 1, pl.ds(PAD + r, ROWS), :])

    def add_total(n, z):
        for r, here in chunks():
            out = pl.ds(r, ROWS)
            new = sum(st[0, c, z, here, :] * st[1, c, z, here, :] for c in range(3))
            tot_ref[z, out, :] = jnp.where(n == 0, 0.0, tot_ref[z, out, :]) + new

    def make_coef():
        @pl.loop(1, GROUPS)
        def _(d):
            src = peer_of(d)
            peer_copy(dens_ref, gath.at[own_rows(src, 0, OWN), :], ga_s.at[d], ga_r.at[src], src).wait_recv()

        @pl.loop(0, depth)
        def _(z):
            rows = jnp.concatenate(
                [gath[pl.ds(z * block_rows + j, blocks, stride=OWN), :] for j in range(block_rows)], axis=0
            )
            smooth = jnp.dot(wmat[...], filter_y(rows), precision=HIGHEST, preferred_element_type=jnp.float32)
            coef_ref[z] = 0.5 / (base[...] + 3.0 * smooth)

    scale = 3.0 / (STEPS * math.sqrt(GROUPS))

    def pack_sums(z, place):
        back = jnp.dot(wtr[...], filter_y(tot_ref[z]), precision=HIGHEST, preferred_element_type=jnp.float32) * scale
        for j in range(block_rows):
            sendb[pl.ds(place * block_rows + j, blocks, stride=OWN), :] = back[j * blocks : (j + 1) * blocks]

    def forward(ev, n):
        @pl.when(relay_up)
        def _():
            u2_via(ev, n, rel.at[ev, n]).wait_recv()
            relay_e_up(ev, n).start()

            @pl.when(n == 0)
            def _():
                h2_via(ev, relh.at[ev]).wait_recv()
                relay_h_up(ev).start()

        @pl.when(relay_dn)
        def _():
            d2_via(ev, n, rel.at[ev, n]).wait_recv()
            relay_e_dn(ev, n).start()

    def edges(ev, n, sending):
        @pl.when(has_up)
        def _():
            d1(ev, n, sdn.at[ev, n, 0]).wait_recv()
            d2(ev, n, sdn.at[ev, n, 1]).wait_recv()

        h_layer(ev, top, lambda r: (eu[ev, n, 0, pl.ds(r, ROWS), :], eu[ev, n, 1, pl.ds(r, ROWS), :]))
        e_layer(ev, n, top, below(ev, top), sup.at[ev, n])
        if sending:

            @pl.when(has_up)
            def _():
                @pl.when(mid_low)
                def _():
                    u2_via(ev, n + 1, sup.at[ev, n, 2]).start()

                @pl.when(jnp.logical_not(mid_low))
                def _():
                    u2(ev, n + 1, sup.at[ev, n, 2]).start()

                u1(ev, n + 1, sup.at[ev, n, 0:2]).start()

        @pl.when(has_dn)
        def _():
            u1(ev, n, sup.at[ev, n, 0:2]).wait_recv()
            u2(ev, n, sup.at[ev, n, 2]).wait_recv()

            @pl.when(n == 0)
            def _():
                h1(ev, ha0.at[ev, 1]).wait_recv()
                h2(ev, ha0.at[ev, 0]).wait_recv()
                ha[ev] = ha0[ev]

            for r, here in chunks():
                out, ahead = pl.ds(r, ROWS), pl.ds(r + 1, ROWS)
                ex, ey, ez = (el[ev, n, c, out, :] for c in range(3))
                ha[ev, 0, out, :] += -COURANT * ((next_y(ez) - ez) - (st[ev, 1, 0, here, :] - ey))
                ha[ev, 1, out, :] += -COURANT * ((st[ev, 0, 0, here, :] - ex) - (el[ev, n, 2, ahead, :] - ez))

        e_layer(ev, n, 0, lambda r: (ha[ev, 0, pl.ds(r, ROWS), :], ha[ev, 1, pl.ds(r, ROWS), :]), sdn.at[ev, n])
        if sending:

            @pl.when(has_dn)
            def _():
                d1(ev, n + 1, sdn.at[ev, n, 0]).start()

                @pl.when(mid_high)
                def _():
                    d2_via(ev, n + 1, sdn.at[ev, n, 1]).start()

                @pl.when(jnp.logical_not(mid_high))
                def _():
                    d2(ev, n + 1, sdn.at[ev, n, 1]).start()

        forward(ev, n)

    @pl.loop(0, 2 * STEPS)
    def _(i):
        n, ev = i // 2, lax.rem(i, 2)

        @pl.when(n == 0)
        def _():
            pltpu.make_async_copy(fwd_ref.at[0], st.at[ev, :, :, inner, :], load_sem.at[ev]).wait()

        h_inside(ev, 0)
        h_inside(ev, top - 1)

        @pl.when(i == 0)
        def _():
            make_coef()

        @pl.when(n < STEPS - 1)
        def _():
            edges(ev, n, True)

        @pl.loop(1, top - 1)
        def _(z):
            h_inside(ev, z)

        @pl.loop(1, top)
        def _(z):
            e_layer(ev, n, z, below(ev, z))

        @pl.when(ev == 1)
        def _():
            @pl.loop(1, top)
            def _(z):
                add_total(n, z)

        @pl.when(i == 2 * STEPS - 1)
        def _():
            @pl.loop(1, top)
            def _(z):
                pack_sums(z, z - 1)

            @pl.loop(1, GROUPS)
            def _(d):
                sums_copy(d, 0, INNER, ri_s, ri_r).start()

        @pl.when(n == STEPS - 1)
        def _():
            edges(ev, n, False)

        @pl.when(ev == 1)
        def _():
            add_total(n, 0)
            add_total(n, top)

        @pl.when(i == 2 * STEPS - 2)
        def _():
            pltpu.make_async_copy(st.at[0, :, :, inner, :], out_ref.at[0], store_sem).start()

    pack_sums(0, top - 1)
    pack_sums(top, top)

    @pl.loop(1, GROUPS)
    def _(d):
        sums_copy(d, INNER, OWN - INNER, rb_s, rb_r).start()

    def arrived(first, count, send, recv):
        def add(d, acc):
            src = peer_of(d)
            rows = own_rows(src, first, count)
            peer_copy(sendb.at[rows, :], recvb.at[rows, :], send.at[d], recv.at[src], src).wait_recv()
            return acc + recvb[rows, :]

        return lax.fori_loop(1, GROUPS, add, sendb[own_rows(grp, first, count), :])

    middle = arrived(0, INNER, ri_s, ri_r)
    for z in range(1, top):
        grad_ref[z * block_rows : (z + 1) * block_rows, :] = middle[(z - 1) * block_rows : z * block_rows]
    ends = arrived(INNER, OWN - INNER, rb_s, rb_r)
    grad_ref[0:block_rows, :] = ends[:block_rows]
    grad_ref[top * block_rows : depth * block_rows, :] = ends[block_rows:]

    pltpu.make_async_copy(st.at[0, :, :, inner, :], out_ref.at[0], store_sem).wait()

    @pl.loop(1, GROUPS)
    def _(d):
        gather_copy(d).wait_send()
        sums_copy(d, 0, INNER, ri_s, ri_r).wait_send()
        sums_copy(d, INNER, OWN - INNER, rb_s, rb_r).wait_send()

    @pl.loop(0, 2)
    def _(ev):
        @pl.when(has_up)
        def _():
            h1(ev, ha0.at[ev, 1]).wait_send()
            h2(ev, ha0.at[ev, 0]).wait_send()

        @pl.when(relay_up)
        def _():
            relay_h_up(ev).wait_send()

        @pl.loop(0, STEPS)
        def _(n):
            @pl.when(has_up)
            def _():
                u1(ev, n, sup.at[ev, n, 0:2]).wait_send()
                u2(ev, n, sup.at[ev, n, 2]).wait_send()

            @pl.when(has_dn)
            def _():
                d1(ev, n, sdn.at[ev, n, 0]).wait_send()
                d2(ev, n, sdn.at[ev, n, 1]).wait_send()

            @pl.when(relay_up)
            def _():
                relay_e_up(ev, n).wait_send()

            @pl.when(relay_dn)
            def _():
                relay_e_dn(ev, n).wait_send()


def per_device(
    fwd_fields, adj_fields, density, block_ids, material_idx, material_eps, source_pos, wave_idx
):
    depth, width_x, width_y = fwd_fields.shape[2:]
    f32 = jnp.float32
    layer = (width_x, width_y)
    rows = density.shape[0] * density.shape[1]
    smem = pl.BlockSpec(memory_space=pltpu.SMEM)
    vmem = pl.BlockSpec(memory_space=pltpu.VMEM)
    hbm = pl.BlockSpec(memory_space=pl.ANY)
    dma = pltpu.SemaphoreType.DMA
    steps, both, peers = dma((2, STEPS)), dma((2,)), dma((GROUPS,))
    finals, grad = pl.pallas_call(
        evolve_kernel,
        out_shape=(jax.ShapeDtypeStruct(fwd_fields.shape, f32), jax.ShapeDtypeStruct((rows, width_y), f32)),
        in_specs=[smem] * 5 + [vmem, hbm, hbm],
        out_specs=(hbm, vmem),
        scratch_shapes=[
            pltpu.VMEM((2, 6, depth, width_x + 2 * PAD, width_y), f32),
            pltpu.VMEM((depth, *layer), f32),
            pltpu.VMEM((depth, *layer), f32),
            pltpu.VMEM((2, STEPS, 3, width_x + PAD, width_y), f32),
            pltpu.VMEM((2, STEPS, 2, *layer), f32),
            pltpu.VMEM((2, 2, *layer), f32),
            pltpu.VMEM((2, 2, *layer), f32),
            pltpu.VMEM((2, STEPS, 3, *layer), f32),
            pltpu.VMEM((2, STEPS, 2, *layer), f32),
            pltpu.VMEM((STEPS, *layer), f32),
            pltpu.VMEM((2, STEPS, *layer), f32),
            pltpu.VMEM((2, *layer), f32),
            pltpu.VMEM((GROUPS * OWN, width_y), f32),
            pltpu.VMEM((GROUPS * OWN, width_y), f32),
            pltpu.VMEM((GROUPS * OWN, width_y), f32),
            pltpu.VMEM(layer, f32),
            pltpu.VMEM(layer, f32),
            pltpu.VMEM(layer, f32),
            both, dma(()),
            steps, steps, steps, steps, both, both, both, both, steps, steps, steps, steps,
            steps, steps, both, both, peers, peers, peers, peers, peers, peers,
        ],
        compiler_params=pltpu.CompilerParams(collective_id=0, has_side_effects=True, vmem_limit_bytes=48 << 20),
        name="evolve",
    )(source_pos, wave_idx, block_ids, material_idx, material_eps, density.reshape(rows, width_y), fwd_fields, adj_fields)
    return finals, grad.reshape(density.shape)


def solution(mesh):
    placed = (
        P("grp", None, "slab", None, None),
        P("grp", None, "slab", None, None),
        P("slab", "grp", None),
        P(),
        P(),
        P(),
        P("grp", None),
        P("grp"),
    )
    return jax.shard_map(
        per_device,
        mesh=mesh,
        in_specs=placed,
        out_specs=(P("grp", None, "slab", None, None), P("slab", "grp", None)),
        check_vma=False,
    )
```

time: 157 us -> 116 us (0.74)
  Pallas kernels: 46.9 us -> 109 us
  starting transfers between devices: 55.4 us -> 0 us
  waiting for transfers between devices: 30.6 us -> 0 us
  local copies, waits for them, and re-layouts: 15.8 us -> 5.6 us
  other arithmetic: 6.41 us -> 0 us
    pallas_call x1, Pallas kernels: 46.9 us -> 109 us  [per_device(): pl.pallas_call(evolve_kernel, out_shape=(jax.ShapeDtypeStruct(fwd_fields....]
    all_to_all x2 -> x0, starting transfers between devices: 55.4 us -> none  [the longest x1 46.2 us: sum_at_owner(): lax.all_to_all(pieces, axis, split_axis=0, concat_axis=0, tiled=True)]
    all_to_all x2 -> x0, waiting for transfers between devices: 30.6 us -> none  [the longest x1 16.5 us: sum_at_owner(): lax.all_to_all(pieces, axis, split_axis=0, concat_axis=0, tiled=True)]
    scatter x2 -> x0, local copies, waits for them, and re-layouts: 6.37 us -> none  [per_device(): jnp.zeros_like(blocks).at[:, block_ids].set(blocks)]
    gather x1 -> x0, local copies, waits for them, and re-layouts: 2.73 us -> none  [per_device(): filter_xy(total).reshape(depth, nblock, block_rows, width_y)[:, block_ids]]
    reduce_sum x2 -> x0, other arithmetic: 1.89 us -> none  [the longest x1 1.14 us: sum_at_owner(): return arrived.sum(axis=0)]
    broadcast_in_dim x3 -> x0, local copies, waits for them, and re-layouts: 1.78 us -> none  [the longest x1 0.85 us: from_everyone(): copies = jnp.broadcast_to(shard, (lax.axis_size(axis), *shard.shape))]
    add x2 -> x0, other arithmetic: 1.75 us -> none  [filter_xy(): rows = padded[:, :-2] + 2.0 * padded[:, 1:-1] + padded[:, 2:]]
  transfers between devices with their start and end apart: 2 -> 0, of which waited for: 2 -> 0; matrix products, arithmetic and copies ran while one was open for 1% -> 0% of each run, Pallas kernels for 0% -> 0%
where the time goes in v2:
time: 116 us
  Pallas kernels  109 us (94%)
  local copies, waits for them, and re-layouts  5.6 us (5%)
  between operations  1.3 us (1%)
    pallas_call x1, Pallas kernels, per_device(): pl.pallas_call(evolve_kernel, out_shape=(jax.ShapeDtypeStruct(fwd_fields....  109 us
    unnamed x12, local copies, waits for them, and re-layouts  5.6 us

profile of v2, /device:TPU:25, one launch (start us, length us, event | category | flops | bytes accessed | tf_op | source)
XLA Modules:
  0.0 115.7 jit_solution(2391641801163598766)
XLA Ops:
  1.3 0.0 copy-start
  1.3 0.7 copy-done
  2.0 0.0 copy-start.1
  2.0 0.7 copy-done.1
  2.7 0.0 copy-start.2
  2.7 0.7 copy-done.2
  3.3 0.0 copy-start.3
  3.3 0.7 copy-done.3
  4.0 0.0 copy-start.4
  4.0 0.7 copy-done.4
  4.6 108.8 %evolve.1 = (f32[1,6,8,128,128]{4,3,2,1,0:T(8,128)S(1)}, f32[32,128]{1,0:T(8,128)S(1)}) custom-call(s32[1,3]{1,0:T(1,128)S(1)} %copy-done.1, s32[1]{0:T(128)S(6)} %copy.12.wave_ref, s32[32]{0:T(128)S(1)} %copy-done.2, s32[32]{0:T(128)S(1)} %copy-done.3, f32[4]{0:T(128)S(1)} %copy-done.4, f32[32,128]{1,0:T(8,128)S(1)} %bitcast.2, ...), custom_call_target="tpu_custom_call" | custom-call | tf_op jit(solution)/shard_map/evolve/pallas_call | solution.py:495
  113.5 1.7 %copy.13 = f32[1,6,8,128,128]{4,3,2,1,0:T(8,128)} copy(f32[1,6,8,128,128]{4,3,2,1,0:T(8,128)S(1)} %get-tuple-element.8) | data formatting | bytes 6291456
  115.1 0.6 copy.14
Async XLA Ops:
  1.3 0.7 copy-start
  2.0 0.7 copy-start.1
  2.7 0.7 copy-start.2
  3.3 0.7 copy-start.3
  4.0 0.7 copy-start.4

commit v3 on v2

v3 whole, which is shorter than its diff:
```python
import math

import jax
import jax.numpy as jnp
from jax import lax
from jax.experimental import pallas as pl
from jax.experimental.pallas import tpu as pltpu
from jax.sharding import PartitionSpec as P

STEPS = 4
COURANT = 0.5
AMPLITUDE = 4.0
MESH = pl.DeviceIdType.MESH
ROWS = 32
PAD = 8
GROUPS = 32
OWN = 32
INNER = 24


def evolve_kernel(
    pos_hbm, wave_hbm, ids_hbm, mat_hbm, eps_hbm, dens_ref, fwd_ref, adj_ref, out_ref, grad_ref,
    st, coef_ref, tot_ref, pin, eu, pout, sdn, drv, gath, sendb, recvb, wmat, wtr, base,
    pos_ref, wave_ref, ids_ref, mat_ref, eps_ref,
    small_sem, load_sem, store_sem, u_s, u_r, d_s, d_r, ga_s, ga_r, ri_s, ri_r, rb_s, rb_r,
):
    depth, width_x, width_y = coef_ref.shape
    top = depth - 1
    grp, slab = lax.axis_index("grp"), lax.axis_index("slab")
    slabs = lax.axis_size("slab")
    has_up, has_dn = slab < slabs - 1, slab > 0
    inner = pl.ds(PAD, width_x)
    fields = (fwd_ref, adj_ref)

    def copy_to(src, dst, send, recv, to_slab):
        return pltpu.make_async_remote_copy(
            src_ref=src, dst_ref=dst, send_sem=send, recv_sem=recv, device_id=(grp, to_slab), device_id_type=MESH)

    def up_copy(ev, n):
        return copy_to(pout.at[ev, n], pin.at[ev, n], u_s.at[ev, n], u_r.at[ev, n], slab + 1)

    def dn_copy(ev, n, src):
        return copy_to(src, eu.at[ev, n], d_s.at[ev, n], d_r.at[ev, n], slab - 1)

    def peer_copy(src, dst, send, recv, peer):
        return pltpu.make_async_remote_copy(
            src_ref=src, dst_ref=dst, send_sem=send, recv_sem=recv, device_id=(peer, slab), device_id_type=MESH)

    def peer_of(d):
        return lax.rem(grp + d, GROUPS)

    def own_rows(k, first, count):
        return pl.ds(pl.multiple_of(k * OWN + first, 8), count)

    def gather_copy(d):
        return peer_copy(dens_ref, gath.at[own_rows(grp, 0, OWN), :], ga_s.at[d], ga_r.at[grp], peer_of(d))

    def sums_copy(d, first, count, send, recv):
        return peer_copy(sendb.at[own_rows(peer_of(d), first, count), :], recvb.at[own_rows(grp, first, count), :],
                         send.at[d], recv.at[grp], peer_of(d))

    barrier = pltpu.get_barrier_semaphore()

    @pl.loop(1, GROUPS)
    def _(d):
        pl.semaphore_signal(barrier, inc=1, device_id=(peer_of(d), slab), device_id_type=MESH)

    def greet(cond, to_slab):
        @pl.when(cond)
        def _():
            pl.semaphore_signal(barrier, inc=1, device_id=(grp, to_slab), device_id_type=MESH)

    greet(has_up, slab + 1)
    greet(has_dn, slab - 1)
    smalls = [
        pltpu.make_async_copy(src, dst, small_sem.at[i])
        for i, (src, dst) in enumerate(
            ((pos_hbm, pos_ref), (wave_hbm, wave_ref), (ids_hbm, ids_ref), (mat_hbm, mat_ref), (eps_hbm, eps_ref))
        )
    ]
    for copy in smalls:
        copy.start()
    for ev in range(2):
        pltpu.make_async_copy(fields[ev].at[0], st.at[ev, :, :, inner, :], load_sem.at[ev]).start()

    zeros = jnp.zeros((PAD, width_y), jnp.float32)

    @pl.loop(0, depth)
    def _(z):
        for ev in range(2):
            for c in (1, 2):
                st[ev, c, z, PAD + width_x :, :] = zeros
            for c in (4, 5):
                st[ev, c, z, :PAD, :] = zeros

    for copy in smalls:
        copy.wait()
    row = lax.broadcasted_iota(jnp.int32, (width_x, width_y), 0)
    col = lax.broadcasted_iota(jnp.int32, (width_x, width_y), 1)
    dx = (row - pos_ref[0, 1]).astype(jnp.float32) / (width_x / 4.0)
    dy = (col - pos_ref[0, 2]).astype(jnp.float32) / (width_y / 4.0)
    profile = jnp.exp(-0.5 * (dx * dx + dy * dy))
    wave = jnp.full((8, width_y), wave_ref[0], jnp.int32).astype(jnp.float32)
    omega = 2.0 * math.pi / (6.0 + 2.0 * wave)
    for n in range(STEPS):
        drv[n] = (AMPLITUDE * jnp.sin(omega * (n + 1.0)))[:1] * profile

    blocks = ids_ref.shape[0]
    block_rows = width_x // blocks
    slot = lax.rem(col, blocks)
    target = col // blocks
    for k in range(blocks):
        target = target + jnp.where(slot == k, ids_ref[k] * block_rows, 0)
    apart = jnp.abs(row - target)
    weights = jnp.where(apart == 0, 0.5, jnp.where(apart == 1, 0.25, 0.0))
    wmat[...] = jnp.concatenate([weights, weights], axis=1).astype(jnp.bfloat16)
    wtr[...] = jnp.concatenate([weights.T, weights.T], axis=1).astype(jnp.bfloat16)
    part = lax.broadcasted_iota(jnp.int32, (8, width_y), 0) // block_rows
    per_tile = 8 // block_rows
    for tile in range(width_x // 8):
        value = jnp.zeros((8, width_y), jnp.float32)
        for q in range(per_tile):
            value = jnp.where(part == q, eps_ref[mat_ref[tile * per_tile + q]], value)
        base[8 * tile : 8 * tile + 8, :] = value
    lane = lax.broadcasted_iota(jnp.int32, (ROWS, width_y), 1)
    is_first, is_last = lane == 0, lane == width_y - 1

    @pl.when(jnp.logical_not(has_up))
    def _():
        eu[...] = jnp.zeros_like(eu)

    @pl.when(jnp.logical_not(has_dn))
    def _():
        pin[...] = jnp.zeros_like(pin)

    own = pl.ds(pl.multiple_of(grp * OWN, 8), OWN)
    gath[own, :] = dens_ref[...]
    def next_y(v):
        return jnp.where(is_last, 0.0, pltpu.roll(v, width_y - 1, axis=1))

    def prev_y(v):
        return jnp.where(is_first, 0.0, pltpu.roll(v, 1, axis=1))

    def chunks():
        return [(r, pl.ds(PAD + r, ROWS)) for r in range(0, width_x, ROWS)]

    def h_layer(ev, z, above):
        for r, here in chunks():
            ahead = pl.ds(PAD + r + 1, ROWS)
            ex, ey, ez = (st[ev, c, z, here, :] for c in range(3))
            exu, eyu = above(r)
            dyz = next_y(ez) - ez
            dyx = next_y(ex) - ex
            st[ev, 3, z, here, :] += -COURANT * (dyz - (eyu - ey))
            st[ev, 4, z, here, :] += -COURANT * ((exu - ex) - (st[ev, 2, z, ahead, :] - ez))
            st[ev, 5, z, here, :] += -COURANT * ((st[ev, 1, z, ahead, :] - ey) - dyx)

    def top_part(ev, n):
        for r, here in chunks():
            ahead = pl.ds(PAD + r + 1, ROWS)
            ex, ey, ez = (st[ev, c, top, here, :] for c in range(3))
            out = pl.ds(r, ROWS)
            pout[ev, n, 0, out, :] = st[ev, 3, top, here, :] - COURANT * ((next_y(ez) - ez) + ey)
            pout[ev, n, 1, out, :] = st[ev, 4, top, here, :] + COURANT * ((st[ev, 2, top, ahead, :] - ez) + ex)

    def h_top(ev, n):
        for r, here in chunks():
            ahead = pl.ds(PAD + r + 1, ROWS)
            out = pl.ds(r, ROWS)
            ex, ey = (st[ev, c, top, here, :] for c in range(2))
            st[ev, 3, top, here, :] = pout[ev, n, 0, out, :] + COURANT * eu[ev, n, 1, out, :]
            st[ev, 4, top, here, :] = pout[ev, n, 1, out, :] - COURANT * eu[ev, n, 0, out, :]
            st[ev, 5, top, here, :] += -COURANT * ((st[ev, 1, top, ahead, :] - ey) - (next_y(ex) - ex))

    for ev in range(2):
        pltpu.make_async_copy(fields[ev].at[0], st.at[ev, :, :, inner, :], load_sem.at[ev]).wait()
        top_part(ev, 0)
    pl.semaphore_wait(barrier, GROUPS - 1 + has_up.astype(jnp.int32) + has_dn.astype(jnp.int32))

    def send_first(ev):
        @pl.when(has_dn)
        def _():
            dn_copy(ev, 0, fields[ev].at[0, 0:2, 0]).start()

        @pl.when(has_up)
        def _():
            up_copy(ev, 0).start()

    send_first(0)

    @pl.loop(1, GROUPS)
    def _(d):
        gather_copy(d).start()

    send_first(1)

    def e_layer(ev, n, z, below, send=None):
        plane = jnp.where((slab * depth + z == pos_ref[0, 0]) & (ev == 0), 1.0, 0.0)
        for r, here in chunks():
            back = pl.ds(PAD + r - 1, ROWS)
            out = pl.ds(r, ROWS)
            hx, hy, hz = (st[ev, c, z, here, :] for c in range(3, 6))
            hxd, hyd = below(r)
            coef = coef_ref[z, out, :]
            ex = st[ev, 0, z, here, :] + coef * ((hz - prev_y(hz)) - (hy - hyd))
            ey = st[ev, 1, z, here, :] + coef * ((hx - hxd) - (hz - st[ev, 5, z, back, :]))
            ez = st[ev, 2, z, here, :] + coef * ((hy - st[ev, 4, z, back, :]) - (hx - prev_y(hx)))
            ez = ez + plane * drv[n, out, :]
            for c, v in enumerate((ex, ey, ez)):
                st[ev, c, z, here, :] = v
            if send is not None:
                for c in range(send.shape[0]):
                    send[c, out, :] = (ex, ey, ez)[c]

    def filter_y(v):
        left = jnp.where(col == 0, 0.0, pltpu.roll(v, 1, axis=1))
        right = jnp.where(col == width_y - 1, 0.0, pltpu.roll(v, width_y - 1, axis=1))
        return (left + 2.0 * v + right) * 0.25

    def mixed(w, v):
        head = v.astype(jnp.bfloat16)
        rest = (v - head.astype(jnp.float32)).astype(jnp.bfloat16)
        return jnp.dot(w[...], jnp.concatenate([head, rest], axis=0), preferred_element_type=jnp.float32)

    def h_inside(ev, z):
        h_layer(ev, z, lambda r: (st[ev, 0, z + 1, pl.ds(PAD + r, ROWS), :], st[ev, 1, z + 1, pl.ds(PAD + r, ROWS), :]))

    def below(ev, z):
        return lambda r: (st[ev, 3, z - 1, pl.ds(PAD + r, ROWS), :], st[ev, 4, z - 1, pl.ds(PAD + r, ROWS), :])

    def add_total(n, z):
        for r, here in chunks():
            out = pl.ds(r, ROWS)
            new = sum(st[0, c, z, here, :] * st[1, c, z, here, :] for c in range(3))
            tot_ref[z, out, :] = jnp.where(n == 0, 0.0, tot_ref[z, out, :]) + new

    def make_coef():
        @pl.loop(1, GROUPS)
        def _(d):
            src = peer_of(d)
            peer_copy(dens_ref, gath.at[own_rows(src, 0, OWN), :], ga_s.at[d], ga_r.at[src], src).wait_recv()

        @pl.loop(0, depth)
        def _(z):
            rows = jnp.concatenate(
                [gath[pl.ds(z * block_rows + j, blocks, stride=OWN), :] for j in range(block_rows)], axis=0
            )
            smooth = mixed(wmat, filter_y(rows))
            coef_ref[z] = 0.5 / (base[...] + 3.0 * smooth)

    scale = 3.0 / (STEPS * math.sqrt(GROUPS))

    def pack_sums(z, place):
        back = mixed(wtr, filter_y(tot_ref[z])) * scale
        for j in range(block_rows):
            sendb[pl.ds(place * block_rows + j, blocks, stride=OWN), :] = back[j * blocks : (j + 1) * blocks]

    half = jnp.where(has_dn, COURANT, 0.0)

    def below_first(ev, n):
        def values(r):
            out, here = pl.ds(r, ROWS), pl.ds(PAD + r, ROWS)
            return (pin[ev, n, 0, out, :] + half * st[ev, 1, 0, here, :], pin[ev, n, 1, out, :] - half * st[ev, 0, 0, here, :])

        return values

    def edges(ev, n, sending):
        @pl.when(has_up)
        def _():
            dn_copy(ev, n, sdn.at[ev, n]).wait_recv()

        h_top(ev, n)
        e_layer(ev, n, top, below(ev, top))
        if sending:
            top_part(ev, n + 1)

            @pl.when(has_up)
            def _():
                up_copy(ev, n + 1).start()

        @pl.when(has_dn)
        def _():
            up_copy(ev, n).wait_recv()

        e_layer(ev, n, 0, below_first(ev, n), sdn.at[ev, n])
        if sending:

            @pl.when(has_dn)
            def _():
                dn_copy(ev, n + 1, sdn.at[ev, n]).start()

    @pl.loop(0, 2 * STEPS)
    def _(i):
        n, ev = i // 2, lax.rem(i, 2)

        h_inside(ev, 0)
        h_inside(ev, top - 1)

        @pl.when(i == 0)
        def _():
            make_coef()

        @pl.when(n < STEPS - 1)
        def _():
            edges(ev, n, True)

        @pl.loop(1, top - 1)
        def _(z):
            h_inside(ev, z)

        @pl.loop(1, top)
        def _(z):
            e_layer(ev, n, z, below(ev, z))

        @pl.when(ev == 1)
        def _():
            @pl.loop(1, top)
            def _(z):
                add_total(n, z)

        @pl.when(i == 2 * STEPS - 1)
        def _():
            @pl.loop(1, top)
            def _(z):
                pack_sums(z, z - 1)

            @pl.loop(1, GROUPS)
            def _(d):
                sums_copy(d, 0, INNER, ri_s, ri_r).start()

        @pl.when(n == STEPS - 1)
        def _():
            edges(ev, n, False)

        @pl.when(ev == 1)
        def _():
            add_total(n, 0)
            add_total(n, top)

        @pl.when(i == 2 * STEPS - 2)
        def _():
            pltpu.make_async_copy(st.at[0, :, :, inner, :], out_ref.at[0], store_sem).start()

    pack_sums(0, top - 1)
    pack_sums(top, top)

    @pl.loop(1, GROUPS)
    def _(d):
        sums_copy(d, INNER, OWN - INNER, rb_s, rb_r).start()

    def arrived(first, count, send, recv):
        def add(d, acc):
            src = peer_of(d)
            rows = own_rows(src, first, count)
            peer_copy(sendb.at[rows, :], recvb.at[rows, :], send.at[d], recv.at[src], src).wait_recv()
            return acc + recvb[rows, :]

        return lax.fori_loop(1, GROUPS, add, sendb[own_rows(grp, first, count), :])

    middle = arrived(0, INNER, ri_s, ri_r)
    for z in range(1, top):
        grad_ref[z * block_rows : (z + 1) * block_rows, :] = middle[(z - 1) * block_rows : z * block_rows]
    ends = arrived(INNER, OWN - INNER, rb_s, rb_r)
    grad_ref[0:block_rows, :] = ends[:block_rows]
    grad_ref[top * block_rows : depth * block_rows, :] = ends[block_rows:]

    pltpu.make_async_copy(st.at[0, :, :, inner, :], out_ref.at[0], store_sem).wait()

    @pl.loop(1, GROUPS)
    def _(d):
        gather_copy(d).wait_send()
        sums_copy(d, 0, INNER, ri_s, ri_r).wait_send()
        sums_copy(d, INNER, OWN - INNER, rb_s, rb_r).wait_send()

    @pl.loop(0, 2)
    def _(ev):
        @pl.loop(0, STEPS)
        def _(n):
            @pl.when(has_up)
            def _():
                up_copy(ev, n).wait_send()

            @pl.when(has_dn)
            def _():
                dn_copy(ev, n, sdn.at[ev, n]).wait_send()


def per_device(
    fwd_fields, adj_fields, density, block_ids, material_idx, material_eps, source_pos, wave_idx
):
    depth, width_x, width_y = fwd_fields.shape[2:]
    f32 = jnp.float32
    layer = (width_x, width_y)
    rows = density.shape[0] * density.shape[1]
    vmem = pl.BlockSpec(memory_space=pltpu.VMEM)
    hbm = pl.BlockSpec(memory_space=pl.ANY)
    dma = pltpu.SemaphoreType.DMA
    steps, peers = dma((2, STEPS)), dma((GROUPS,))
    finals, grad = pl.pallas_call(
        evolve_kernel,
        out_shape=(jax.ShapeDtypeStruct(fwd_fields.shape, f32), jax.ShapeDtypeStruct((rows, width_y), f32)),
        in_specs=[hbm] * 5 + [vmem, hbm, hbm],
        out_specs=(hbm, vmem),
        scratch_shapes=[
            pltpu.VMEM((2, 6, depth, width_x + 2 * PAD, width_y), f32),
            pltpu.VMEM((depth, *layer), f32),
            pltpu.VMEM((depth, *layer), f32),
            pltpu.VMEM((2, STEPS, 2, *layer), f32),
            pltpu.VMEM((2, STEPS, 2, *layer), f32),
            pltpu.VMEM((2, STEPS, 2, *layer), f32),
            pltpu.VMEM((2, STEPS, 2, *layer), f32),
            pltpu.VMEM((STEPS, *layer), f32),
            pltpu.VMEM((GROUPS * OWN, width_y), f32),
            pltpu.VMEM((GROUPS * OWN, width_y), f32),
            pltpu.VMEM((GROUPS * OWN, width_y), f32),
            pltpu.VMEM((width_x, 2 * width_x), jnp.bfloat16),
            pltpu.VMEM((width_x, 2 * width_x), jnp.bfloat16),
            pltpu.VMEM(layer, f32),
            *(pltpu.SMEM(a.shape, a.dtype) for a in (source_pos, wave_idx, block_ids, material_idx, material_eps)),
            dma((5,)), dma((2,)), dma(()), steps, steps, steps, steps, *[peers] * 6,
        ],
        compiler_params=pltpu.CompilerParams(collective_id=0, has_side_effects=True, vmem_limit_bytes=48 << 20),
        name="evolve",
    )(source_pos, wave_idx, block_ids, material_idx, material_eps, density.reshape(rows, width_y), fwd_fields, adj_fields)
    return finals, grad.reshape(density.shape)


def solution(mesh):
    placed = (
        P("grp", None, "slab", None, None),
        P("grp", None, "slab", None, None),
        P("slab", "grp", None),
        P(),
        P(),
        P(),
        P("grp", None),
        P("grp"),
    )
    return jax.shard_map(
        per_device,
        mesh=mesh,
        in_specs=placed,
        out_specs=(P("grp", None, "slab", None, None), P("slab", "grp", None)),
        check_vma=False,
    )
```

time: 116 us -> 89.6 us (0.77)
  Pallas kernels: 109 us -> 82.4 us
    pallas_call x1, Pallas kernels: 109 us -> 82.4 us  [per_device(): pl.pallas_call(evolve_kernel, out_shape=(jax.ShapeDtypeStruct(fwd_fields....]
where the time goes in v3:
time: 89.6 us; the launch traced here: 89.3 us
  Pallas kernels  82.4 us (92%)
  local copies, waits for them, and re-layouts  5.6 us (6%)
  between operations  1.3 us (1%)
    pallas_call x1, Pallas kernels, per_device(): pl.pallas_call(evolve_kernel, out_shape=(jax.ShapeDtypeStruct(fwd_fields....  82.4 us
    unnamed x12, local copies, waits for them, and re-layouts  5.6 us

profile of v3, /device:TPU:25, one launch (start us, length us, event | category | flops | bytes accessed | tf_op | source)
XLA Modules:
  0.0 89.3 jit_solution(2951877992756077969)
XLA Ops:
  1.3 0.0 copy-start
  1.3 0.7 copy-done
  2.0 0.0 copy-start.1
  2.0 0.7 copy-done.1
  2.7 0.0 copy-start.2
  2.7 0.7 copy-done.2
  3.3 0.0 copy-start.3
  3.3 0.7 copy-done.3
  4.0 0.0 copy-start.4
  4.0 0.7 copy-done.4
  4.6 82.4 %evolve.1 = (f32[1,6,8,128,128]{4,3,2,1,0:T(8,128)S(1)}, f32[32,128]{1,0:T(8,128)S(1)}) custom-call(s32[1,3]{1,0:T(1,128)S(1)} %copy-done.1, s32[1]{0:T(128)S(6)} %copy.12.wave_hbm, s32[32]{0:T(128)S(1)} %copy-done.2, s32[32]{0:T(128)S(1)} %copy-done.3, f32[4]{0:T(128)S(1)} %copy-done.4, f32[32,128]{1,0:T(8,128)S(1)} %bitcast.2, ...), custom_call_target="tpu_custom_call" | custom-call | tf_op jit(solution)/shard_map/evolve/pallas_call | solution.py:399
  87.1 1.7 %copy.13 = f32[1,6,8,128,128]{4,3,2,1,0:T(8,128)} copy(f32[1,6,8,128,128]{4,3,2,1,0:T(8,128)S(1)} %get-tuple-element.8) | data formatting | bytes 6291456
  88.7 0.6 copy.14
Async XLA Ops:
  1.3 0.7 copy-start
  2.0 0.7 copy-start.1
  2.7 0.7 copy-start.2
  3.3 0.7 copy-start.3
  4.0 0.7 copy-start.4

commit v4 on v3

--- a/solution.py
+++ b/solution.py
@@ -16,19 +16,29 @@
 GROUPS = 32
 OWN = 32
 INNER = 24
+EDGE = 8
+LINE = 8
+COLUMNS = 4
 
 
 def evolve_kernel(
     pos_hbm, wave_hbm, ids_hbm, mat_hbm, eps_hbm, dens_ref, fwd_ref, adj_ref, out_ref, grad_ref,
-    st, coef_ref, tot_ref, pin, eu, pout, sdn, drv, gath, sendb, recvb, wmat, wtr, base,
+    st, coef_ref, tot_ref, pin, eu, pout, sdn, rel, drv, gath, mine, column, line, edge, edge_in, wmat, wtr, base,
     pos_ref, wave_ref, ids_ref, mat_ref, eps_ref,
-    small_sem, load_sem, store_sem, u_s, u_r, d_s, d_r, ga_s, ga_r, ri_s, ri_r, rb_s, rb_r,
+    small_sem, load_sem, store_sem, own_sem, u1_s, u1_r, u2_s, u2_r, d1_s, d1_r, d2_s, d2_r, rl_s, rl_r,
+    gl_s, gl_r, gc_s, gc_r, sc_s, sc_r, sl_s, sl_r, se_s, se_r,
 ):
     depth, width_x, width_y = coef_ref.shape
     top = depth - 1
     grp, slab = lax.axis_index("grp"), lax.axis_index("slab")
     slabs = lax.axis_size("slab")
-    has_up, has_dn = slab < slabs - 1, slab > 0
+    last = slabs - 1
+    low, high = slabs // 2 - 1, slabs // 2
+    has_up, has_dn = slab < last, slab > 0
+    run, col_x, core = grp // LINE, lax.rem(grp // 2, COLUMNS), lax.rem(grp, 2)
+    place = run * 2 + core
+    far_low, far_high = slab == low, slab == high
+    relay_up, relay_dn = slab == 0, slab == last
     inner = pl.ds(PAD, width_x)
     fields = (fwd_ref, adj_ref)
 
@@ -36,11 +46,66 @@
         return pltpu.make_async_remote_copy(
             src_ref=src, dst_ref=dst, send_sem=send, recv_sem=recv, device_id=(grp, to_slab), device_id_type=MESH)
 
-    def up_copy(ev, n):
-        return copy_to(pout.at[ev, n], pin.at[ev, n], u_s.at[ev, n], u_r.at[ev, n], slab + 1)
-
-    def dn_copy(ev, n, src):
-        return copy_to(src, eu.at[ev, n], d_s.at[ev, n], d_r.at[ev, n], slab - 1)
+    def u1(ev, n):
+        return copy_to(pout.at[ev, n, 0], pin.at[ev, n, 0], u1_s.at[ev, n], u1_r.at[ev, n], slab + 1)
+
+    def u2(ev, n):
+        return copy_to(pout.at[ev, n, 1], pin.at[ev, n, 1], u2_s.at[ev, n], u2_r.at[ev, n], slab + 1)
+
+    def u2_via(ev, n):
+        return copy_to(pout.at[ev, n, 1], rel.at[ev, n], u2_s.at[ev, n], rl_r.at[ev, n], 0)
+
+    def relay_u2(ev, n):
+        return copy_to(rel.at[ev, n], pin.at[ev, n, 1], rl_s.at[ev, n], u2_r.at[ev, n], high)
+
+    def d1(ev, n, src):
+        return copy_to(src, eu.at[ev, n, 0], d1_s.at[ev, n], d1_r.at[ev, n], slab - 1)
+
+    def d2(ev, n, src):
+        return copy_to(src, eu.at[ev, n, 1], d2_s.at[ev, n], d2_r.at[ev, n], slab - 1)
+
+    def d2_via(ev, n, src):
+        return copy_to(src, rel.at[ev, n], d2_s.at[ev, n], rl_r.at[ev, n], last)
+
+    def relay_d2(ev, n):
+        return copy_to(rel.at[ev, n], eu.at[ev, n, 1], rl_s.at[ev, n], d2_r.at[ev, n], low)
+
+    def send_up(ev, n):
+        @pl.when(has_up)
+        def _():
+            @pl.when(far_low)
+            def _():
+                u2_via(ev, n).start()
+
+            @pl.when(jnp.logical_not(far_low))
+            def _():
+                u2(ev, n).start()
+
+            u1(ev, n).start()
+
+    def send_dn(ev, n, first, second):
+        @pl.when(has_dn)
+        def _():
+            @pl.when(far_high)
+            def _():
+                d2_via(ev, n, second).start()
+
+            @pl.when(jnp.logical_not(far_high))
+            def _():
+                d2(ev, n, second).start()
+
+            d1(ev, n, first).start()
+
+    def forward(ev, n):
+        @pl.when(relay_up)
+        def _():
+            u2_via(ev, n).wait_recv()
+            relay_u2(ev, n).start()
+
+        @pl.when(relay_dn)
+        def _():
+            d2_via(ev, n, rel.at[ev, n]).wait_recv()
+            relay_d2(ev, n).start()
 
     def peer_copy(src, dst, send, recv, peer):
         return pltpu.make_async_remote_copy(
@@ -49,15 +114,42 @@
     def peer_of(d):
         return lax.rem(grp + d, GROUPS)
 
-    def own_rows(k, first, count):
-        return pl.ds(pl.multiple_of(k * OWN + first, 8), count)
-
-    def gather_copy(d):
-        return peer_copy(dens_ref, gath.at[own_rows(grp, 0, OWN), :], ga_s.at[d], ga_r.at[grp], peer_of(d))
-
-    def sums_copy(d, first, count, send, recv):
-        return peer_copy(sendb.at[own_rows(peer_of(d), first, count), :], recvb.at[own_rows(grp, first, count), :],
-                         send.at[d], recv.at[grp], peer_of(d))
+    def rows_of(k, count):
+        return pl.ds(pl.multiple_of(k * count, 8), count)
+
+    def slot_of(g):
+        return lax.rem(g // 2, COLUMNS) * LINE + (g // LINE) * 2 + lax.rem(g, 2)
+
+    def line_peer(q):
+        other = lax.rem(place + q, LINE)
+        return other, (other // 2) * LINE + col_x * 2 + lax.rem(other, 2)
+
+    def column_peer(p):
+        other = lax.rem(col_x + p, COLUMNS)
+        return other, run * LINE + other * 2 + core
+
+    def gather_line(q, sender):
+        rows = gath.at[rows_of(col_x * LINE + sender, OWN), :]
+        return peer_copy(dens_ref, rows, gl_s.at[q], gl_r.at[sender], line_peer(q)[1])
+
+    def gather_column(p, sender):
+        rows = gath.at[rows_of(sender, LINE * OWN), :]
+        return peer_copy(rows, rows, gc_s.at[p], gc_r.at[sender], column_peer(p)[1])
+
+    def sums_column(p, sender):
+        other, peer = column_peer(p)
+        return peer_copy(mine.at[rows_of(other, LINE * INNER), :], column.at[rows_of(sender, LINE * INNER), :],
+                         sc_s.at[p], sc_r.at[sender], peer)
+
+    def sums_line(q, sender):
+        other, peer = line_peer(q)
+        kept = rows_of(col_x * LINE + other, INNER)
+        return peer_copy(mine.at[kept, :], line.at[rows_of(sender, INNER), :], sl_s.at[q], sl_r.at[sender], peer)
+
+    def sums_edge(d, sender):
+        peer = peer_of(d)
+        return peer_copy(edge.at[rows_of(slot_of(peer), EDGE), :], edge_in.at[rows_of(slot_of(sender), EDGE), :],
+                         se_s.at[d], se_r.at[sender], peer)
 
     barrier = pltpu.get_barrier_semaphore()
 
@@ -72,6 +164,10 @@
 
     greet(has_up, slab + 1)
     greet(has_dn, slab - 1)
+    greet(far_low | far_high, 0)
+    greet(far_low | far_high, last)
+    greet(relay_up | relay_dn, low)
+    greet(relay_up | relay_dn, high)
     smalls = [
         pltpu.make_async_copy(src, dst, small_sem.at[i])
         for i, (src, dst) in enumerate(
@@ -80,6 +176,8 @@
     ]
     for copy in smalls:
         copy.start()
+    own_copy = pltpu.make_async_copy(dens_ref, gath.at[rows_of(slot_of(grp), OWN), :], own_sem)
+    own_copy.start()
     for ev in range(2):
         pltpu.make_async_copy(fields[ev].at[0], st.at[ev, :, :, inner, :], load_sem.at[ev]).start()
 
@@ -110,7 +208,8 @@
     slot = lax.rem(col, blocks)
     target = col // blocks
     for k in range(blocks):
-        target = target + jnp.where(slot == k, ids_ref[k] * block_rows, 0)
+        here = (k // 2 % COLUMNS) * LINE + (k // LINE) * 2 + k % 2
+        target = target + jnp.where(slot == here, ids_ref[k] * block_rows, 0)
     apart = jnp.abs(row - target)
     weights = jnp.where(apart == 0, 0.5, jnp.where(apart == 1, 0.25, 0.0))
     wmat[...] = jnp.concatenate([weights, weights], axis=1).astype(jnp.bfloat16)
@@ -133,8 +232,6 @@
     def _():
         pin[...] = jnp.zeros_like(pin)
 
-    own = pl.ds(pl.multiple_of(grp * OWN, 8), OWN)
-    gath[own, :] = dens_ref[...]
     def next_y(v):
         return jnp.where(is_last, 0.0, pltpu.roll(v, width_y - 1, axis=1))
 
@@ -175,24 +272,15 @@
     for ev in range(2):
         pltpu.make_async_copy(fields[ev].at[0], st.at[ev, :, :, inner, :], load_sem.at[ev]).wait()
         top_part(ev, 0)
-    pl.semaphore_wait(barrier, GROUPS - 1 + has_up.astype(jnp.int32) + has_dn.astype(jnp.int32))
-
-    def send_first(ev):
-        @pl.when(has_dn)
-        def _():
-            dn_copy(ev, 0, fields[ev].at[0, 0:2, 0]).start()
-
-        @pl.when(has_up)
-        def _():
-            up_copy(ev, 0).start()
-
-    send_first(0)
-
-    @pl.loop(1, GROUPS)
-    def _(d):
-        gather_copy(d).start()
-
-    send_first(1)
+    extra = jnp.where(far_low | far_high | relay_up | relay_dn, 2, 0)
+    pl.semaphore_wait(barrier, GROUPS - 1 + has_up.astype(jnp.int32) + has_dn.astype(jnp.int32) + extra)
+
+    @pl.loop(1, LINE)
+    def _(q):
+        gather_line(q, place).start()
+
+    send_dn(0, 0, fwd_ref.at[0, 0, 0], fwd_ref.at[0, 1, 0])
+    send_up(0, 0)
 
     def e_layer(ev, n, z, below, send=None):
         plane = jnp.where((slab * depth + z == pos_ref[0, 0]) & (ev == 0), 1.0, 0.0)
@@ -234,26 +322,38 @@
             new = sum(st[0, c, z, here, :] * st[1, c, z, here, :] for c in range(3))
             tot_ref[z, out, :] = jnp.where(n == 0, 0.0, tot_ref[z, out, :]) + new
 
-    def make_coef():
-        @pl.loop(1, GROUPS)
-        def _(d):
-            src = peer_of(d)
-            peer_copy(dens_ref, gath.at[own_rows(src, 0, OWN), :], ga_s.at[d], ga_r.at[src], src).wait_recv()
-
-        @pl.loop(0, depth)
-        def _(z):
-            rows = jnp.concatenate(
-                [gath[pl.ds(z * block_rows + j, blocks, stride=OWN), :] for j in range(block_rows)], axis=0
-            )
-            smooth = mixed(wmat, filter_y(rows))
-            coef_ref[z] = 0.5 / (base[...] + 3.0 * smooth)
+    def gather():
+        own_copy.wait()
+
+        @pl.loop(1, LINE)
+        def _(q):
+            gather_line(q, line_peer(q)[0]).wait_recv()
+
+        @pl.loop(1, COLUMNS)
+        def _(p):
+            gather_column(p, col_x).start()
+
+        send_dn(1, 0, adj_ref.at[0, 0, 0], adj_ref.at[0, 1, 0])
+        send_up(1, 0)
+        forward(0, 0)
+        forward(1, 0)
+
+        @pl.loop(1, COLUMNS)
+        def _(p):
+            gather_column(p, column_peer(p)[0]).wait_recv()
+
+    def make_coef(z):
+        rows = jnp.concatenate(
+            [gath[pl.ds(z * block_rows + j, blocks, stride=OWN), :] for j in range(block_rows)], axis=0
+        )
+        coef_ref[z] = 0.5 / (base[...] + 3.0 * mixed(wmat, filter_y(rows)))
 
     scale = 3.0 / (STEPS * math.sqrt(GROUPS))
 
-    def pack_sums(z, place):
+    def pack_sums(z, packed, first, count):
         back = mixed(wtr, filter_y(tot_ref[z])) * scale
         for j in range(block_rows):
-            sendb[pl.ds(place * block_rows + j, blocks, stride=OWN), :] = back[j * blocks : (j + 1) * blocks]
+            packed[pl.ds(first + j, blocks, stride=count), :] = back[j * blocks : (j + 1) * blocks]
 
     half = jnp.where(has_dn, COURANT, 0.0)
 
@@ -267,110 +367,143 @@
     def edges(ev, n, sending):
         @pl.when(has_up)
         def _():
-            dn_copy(ev, n, sdn.at[ev, n]).wait_recv()
+            d1(ev, n, sdn.at[ev, n, 0]).wait_recv()
+            d2(ev, n, sdn.at[ev, n, 1]).wait_recv()
 
         h_top(ev, n)
         e_layer(ev, n, top, below(ev, top))
         if sending:
             top_part(ev, n + 1)
-
-            @pl.when(has_up)
-            def _():
-                up_copy(ev, n + 1).start()
+            send_up(ev, n + 1)
 
         @pl.when(has_dn)
         def _():
-            up_copy(ev, n).wait_recv()
+            u1(ev, n).wait_recv()
+            u2(ev, n).wait_recv()
 
         e_layer(ev, n, 0, below_first(ev, n), sdn.at[ev, n])
         if sending:
-
-            @pl.when(has_dn)
-            def _():
-                dn_copy(ev, n + 1, sdn.at[ev, n]).start()
-
-    @pl.loop(0, 2 * STEPS)
-    def _(i):
-        n, ev = i // 2, lax.rem(i, 2)
-
-        h_inside(ev, 0)
-        h_inside(ev, top - 1)
-
-        @pl.when(i == 0)
-        def _():
-            make_coef()
-
-        @pl.when(n < STEPS - 1)
-        def _():
-            edges(ev, n, True)
-
-        @pl.loop(1, top - 1)
+            send_dn(ev, n + 1, sdn.at[ev, n, 0], sdn.at[ev, n, 1])
+
+            @pl.when(n > 0)
+            def _():
+                forward(ev, n)
+
+    def h_rest(ev):
+        @pl.loop(0, top)
         def _(z):
             h_inside(ev, z)
 
+    def e_rest(ev, n):
         @pl.loop(1, top)
         def _(z):
             e_layer(ev, n, z, below(ev, z))
 
-        @pl.when(ev == 1)
+    @pl.loop(0, 2 * STEPS - 2)
+    def _(i):
+        n, ev = i // 2, lax.rem(i, 2)
+        h_rest(ev)
+
+        @pl.when(i == 0)
+        def _():
+            gather()
+            make_coef(0)
+            make_coef(top)
+
+        edges(ev, n, True)
+
+        @pl.when(i == 0)
         def _():
             @pl.loop(1, top)
             def _(z):
+                make_coef(z)
+
+        e_rest(ev, n)
+
+        @pl.when(ev == 1)
+        def _():
+            @pl.loop(0, depth)
+            def _(z):
                 add_total(n, z)
 
-        @pl.when(i == 2 * STEPS - 1)
-        def _():
-            @pl.loop(1, top)
-            def _(z):
-                pack_sums(z, z - 1)
-
-            @pl.loop(1, GROUPS)
-            def _(d):
-                sums_copy(d, 0, INNER, ri_s, ri_r).start()
-
-        @pl.when(n == STEPS - 1)
-        def _():
-            edges(ev, n, False)
-
-        @pl.when(ev == 1)
-        def _():
-            add_total(n, 0)
-            add_total(n, top)
-
-        @pl.when(i == 2 * STEPS - 2)
+    n = STEPS - 1
+
+    @pl.loop(0, 2)
+    def _(ev):
+        h_rest(ev)
+        e_rest(ev, n)
+
+    @pl.loop(1, top)
+    def _(z):
+        add_total(n, z)
+        pack_sums(z, mine, (z - 1) * block_rows, INNER)
+
+    @pl.loop(1, COLUMNS)
+    def _(p):
+        sums_column(p, col_x).start()
+
+    @pl.loop(0, 2)
+    def _(ev):
+        forward(ev, n)
+        edges(ev, n, False)
+
+        @pl.when(ev == 0)
         def _():
             pltpu.make_async_copy(st.at[0, :, :, inner, :], out_ref.at[0], store_sem).start()
 
-    pack_sums(0, top - 1)
-    pack_sums(top, top)
+            @pl.loop(1, COLUMNS)
+            def _(p):
+                sender = column_peer(p)[0]
+                sums_column(p, sender).wait_recv()
+                kept = rows_of(col_x, LINE * INNER)
+                mine[kept, :] += column[rows_of(sender, LINE * INNER), :]
+
+            @pl.loop(1, LINE)
+            def _(q):
+                sums_line(q, place).start()
+
+    add_total(n, 0)
+    add_total(n, top)
+    pack_sums(0, edge, 0, EDGE)
+    pack_sums(top, edge, block_rows, EDGE)
 
     @pl.loop(1, GROUPS)
     def _(d):
-        sums_copy(d, INNER, OWN - INNER, rb_s, rb_r).start()
-
-    def arrived(first, count, send, recv):
-        def add(d, acc):
-            src = peer_of(d)
-            rows = own_rows(src, first, count)
-            peer_copy(sendb.at[rows, :], recvb.at[rows, :], send.at[d], recv.at[src], src).wait_recv()
-            return acc + recvb[rows, :]
-
-        return lax.fori_loop(1, GROUPS, add, sendb[own_rows(grp, first, count), :])
-
-    middle = arrived(0, INNER, ri_s, ri_r)
+        sums_edge(d, grp).start()
+
+    def add_line(q, acc):
+        sender = line_peer(q)[0]
+        sums_line(q, sender).wait_recv()
+        return acc + line[rows_of(sender, INNER), :]
+
+    middle = lax.fori_loop(1, LINE, add_line, mine[rows_of(slot_of(grp), INNER), :])
     for z in range(1, top):
         grad_ref[z * block_rows : (z + 1) * block_rows, :] = middle[(z - 1) * block_rows : z * block_rows]
-    ends = arrived(INNER, OWN - INNER, rb_s, rb_r)
+
+    def add_edge(d, acc):
+        sender = peer_of(d)
+        sums_edge(d, sender).wait_recv()
+        return acc + edge_in[rows_of(slot_of(sender), EDGE), :]
+
+    ends = lax.fori_loop(1, GROUPS, add_edge, edge[rows_of(slot_of(grp), EDGE), :])
     grad_ref[0:block_rows, :] = ends[:block_rows]
     grad_ref[top * block_rows : depth * block_rows, :] = ends[block_rows:]
 
     pltpu.make_async_copy(st.at[0, :, :, inner, :], out_ref.at[0], store_sem).wait()
 
+    @pl.loop(1, LINE)
+    def _(q):
+        gather_line(q, place).wait_send()
+        sums_line(q, place).wait_send()
+
+    @pl.loop(1, COLUMNS)
+    def _(p):
+        gather_column(p, col_x).wait_send()
+        sums_column(p, col_x).wait_send()
+
     @pl.loop(1, GROUPS)
     def _(d):
-        gather_copy(d).wait_send()
-        sums_copy(d, 0, INNER, ri_s, ri_r).wait_send()
-        sums_copy(d, INNER, OWN - INNER, rb_s, rb_r).wait_send()
+        sums_edge(d, grp).wait_send()
 
     @pl.loop(0, 2)
     def _(ev):
@@ -378,11 +511,21 @@
         def _(n):
             @pl.when(has_up)
             def _():
-                up_copy(ev, n).wait_send()
+                u1(ev, n).wait_send()
+                u2(ev, n).wait_send()
 
             @pl.when(has_dn)
             def _():
-                dn_copy(ev, n, sdn.at[ev, n]).wait_send()
+                d1(ev, n, sdn.at[ev, n, 0]).wait_send()
+                d2(ev, n, sdn.at[ev, n, 1]).wait_send()
+
+            @pl.when(relay_up)
+            def _():
+                relay_u2(ev, n).wait_send()
+
+            @pl.when(relay_dn)
+            def _():
+                relay_d2(ev, n).wait_send()
 
 
 def per_device(
@@ -393,14 +536,15 @@
     layer = (width_x, width_y)
     rows = density.shape[0] * density.shape[1]
     vmem = pl.BlockSpec(memory_space=pltpu.VMEM)
-    hbm = pl.BlockSpec(memory_space=pl.ANY)
+    anywhere = pl.BlockSpec(memory_space=pl.ANY)
+    hbm = pl.BlockSpec(memory_space=pltpu.HBM)
     dma = pltpu.SemaphoreType.DMA
-    steps, peers = dma((2, STEPS)), dma((GROUPS,))
+    steps = dma((2, STEPS))
     finals, grad = pl.pallas_call(
         evolve_kernel,
         out_shape=(jax.ShapeDtypeStruct(fwd_fields.shape, f32), jax.ShapeDtypeStruct((rows, width_y), f32)),
-        in_specs=[hbm] * 5 + [vmem, hbm, hbm],
-        out_specs=(hbm, vmem),
+        in_specs=[hbm] * 8,
+        out_specs=(anywhere, vmem),
         scratch_shapes=[
             pltpu.VMEM((2, 6, depth, width_x + 2 * PAD, width_y), f32),
             pltpu.VMEM((depth, *layer), f32),
@@ -409,15 +553,20 @@
             pltpu.VMEM((2, STEPS, 2, *layer), f32),
             pltpu.VMEM((2, STEPS, 2, *layer), f32),
             pltpu.VMEM((2, STEPS, 2, *layer), f32),
+            pltpu.VMEM((2, STEPS, *layer), f32),
             pltpu.VMEM((STEPS, *layer), f32),
             pltpu.VMEM((GROUPS * OWN, width_y), f32),
-            pltpu.VMEM((GROUPS * OWN, width_y), f32),
-            pltpu.VMEM((GROUPS * OWN, width_y), f32),
+            pltpu.VMEM((GROUPS * INNER, width_y), f32),
+            pltpu.VMEM((GROUPS * INNER, width_y), f32),
+            pltpu.VMEM((LINE * INNER, width_y), f32),
+            pltpu.VMEM((GROUPS * EDGE, width_y), f32),
+            pltpu.VMEM((GROUPS * EDGE, width_y), f32),
             pltpu.VMEM((width_x, 2 * width_x), jnp.bfloat16),
             pltpu.VMEM((width_x, 2 * width_x), jnp.bfloat16),
             pltpu.VMEM(layer, f32),
             *(pltpu.SMEM(a.shape, a.dtype) for a in (source_pos, wave_idx, block_ids, material_idx, material_eps)),
-            dma((5,)), dma((2,)), dma(()), steps, steps, steps, steps, *[peers] * 6,
+            dma((5,)), dma((2,)), dma(()), dma(()), *[steps] * 10,
+            *[dma((LINE,))] * 2, *[dma((COLUMNS,))] * 4, *[dma((LINE,))] * 2, *[dma((GROUPS,))] * 2,
         ],
         compiler_params=pltpu.CompilerParams(collective_id=0, has_side_effects=True, vmem_limit_bytes=48 << 20),
         name="evolve",

time: 89.6 us -> 74.5 us (0.83)
  Pallas kernels: 82.4 us -> 67.4 us
    pallas_call x1, Pallas kernels: 82.4 us -> 67.4 us  [per_device(): pl.pallas_call(evolve_kernel, out_shape=(jax.ShapeDtypeStruct(fwd_fields....]
where the time goes in v4:
time: 74.5 us; the launch traced here: 74.3 us
  Pallas kernels  67.4 us (90%)
  local copies, waits for them, and re-layouts  5.6 us (8%)
  between operations  1.3 us (2%)
    pallas_call x1, Pallas kernels, per_device(): pl.pallas_call(evolve_kernel, out_shape=(jax.ShapeDtypeStruct(fwd_fields....  67.4 us
    unnamed x12, local copies, waits for them, and re-layouts  5.6 us

profile of v4, /device:TPU:25, one launch (start us, length us, event | category | flops | bytes accessed | tf_op | source)
XLA Modules:
  0.0 74.3 jit_solution(15058767946564655439)
XLA Ops:
  1.3 0.0 copy-start
  1.3 0.7 copy-done
  2.0 0.0 copy-start.1
  2.0 0.7 copy-done.1
  2.7 0.0 copy-start.2
  2.7 0.7 copy-done.2
  3.3 0.0 copy-start.3
  3.3 0.7 copy-done.3
  4.0 0.0 copy-start.4
  4.0 0.7 copy-done.4
  4.6 67.4 %evolve.1 = (f32[1,6,8,128,128]{4,3,2,1,0:T(8,128)S(1)}, f32[32,128]{1,0:T(8,128)S(1)}) custom-call(s32[1,3]{1,0:T(1,128)S(1)} %copy-done.1, s32[1]{0:T(128)S(6)} %copy.12.wave_hbm, s32[32]{0:T(128)S(1)} %copy-done.2, s32[32]{0:T(128)S(1)} %copy-done.3, f32[4]{0:T(128)S(1)} %copy-done.4, f32[32,128]{1,0:T(8,128)S(1)} %bitcast.2, ...), custom_call_target="tpu_custom_call" | custom-call | tf_op jit(solution)/shard_map/evolve/pallas_call | solution.py:543
  72.0 1.7 %copy.13 = f32[1,6,8,128,128]{4,3,2,1,0:T(8,128)} copy(f32[1,6,8,128,128]{4,3,2,1,0:T(8,128)S(1)} %get-tuple-element.8) | data formatting | bytes 6291456
  73.7 0.6 copy.14
Async XLA Ops:
  1.3 0.7 copy-start
  2.0 0.7 copy-start.1
  2.7 0.7 copy-start.2
  3.3 0.7 copy-start.3
  4.0 0.7 copy-start.4

commit v5 on v4

--- a/solution.py
+++ b/solution.py
@@ -132,9 +132,9 @@
         rows = gath.at[rows_of(col_x * LINE + sender, OWN), :]
         return peer_copy(dens_ref, rows, gl_s.at[q], gl_r.at[sender], line_peer(q)[1])
 
-    def gather_column(p, sender):
-        rows = gath.at[rows_of(sender, LINE * OWN), :]
-        return peer_copy(rows, rows, gc_s.at[p], gc_r.at[sender], column_peer(p)[1])
+    def gather_column(p, sender, which, src=None):
+        rows = gath.at[rows_of(sender * LINE + which, OWN), :]
+        return peer_copy(rows if src is None else src, rows, gc_s.at[p, which], gc_r.at[sender, which], column_peer(p)[1])
 
     def sums_column(p, sender):
         other, peer = column_peer(p)
@@ -149,7 +149,7 @@
     def sums_edge(d, sender):
         peer = peer_of(d)
         return peer_copy(edge.at[rows_of(slot_of(peer), EDGE), :], edge_in.at[rows_of(slot_of(sender), EDGE), :],
-                         se_s.at[d], se_r.at[sender], peer)
+                         se_s, se_r, peer)
 
     barrier = pltpu.get_barrier_semaphore()
 
@@ -279,6 +279,10 @@
     def _(q):
         gather_line(q, place).start()
 
+    @pl.loop(1, COLUMNS)
+    def _(p):
+        gather_column(p, col_x, place, dens_ref).start()
+
     send_dn(0, 0, fwd_ref.at[0, 0, 0], fwd_ref.at[0, 1, 0])
     send_up(0, 0)
 
@@ -327,20 +331,23 @@
 
         @pl.loop(1, LINE)
         def _(q):
-            gather_line(q, line_peer(q)[0]).wait_recv()
-
-        @pl.loop(1, COLUMNS)
-        def _(p):
-            gather_column(p, col_x).start()
+            which = line_peer(q)[0]
+            gather_line(q, which).wait_recv()
+
+            @pl.loop(1, COLUMNS)
+            def _(p):
+                gather_column(p, col_x, which).start()
 
         send_dn(1, 0, adj_ref.at[0, 0, 0], adj_ref.at[0, 1, 0])
         send_up(1, 0)
         forward(0, 0)
         forward(1, 0)
 
-        @pl.loop(1, COLUMNS)
-        def _(p):
-            gather_column(p, column_peer(p)[0]).wait_recv()
+        @pl.loop(0, LINE)
+        def _(which):
+            @pl.loop(1, COLUMNS)
+            def _(p):
+                gather_column(p, column_peer(p)[0], which).wait_recv()
 
     def make_coef(z):
         rows = jnp.concatenate(
@@ -385,19 +392,19 @@
         if sending:
             send_dn(ev, n + 1, sdn.at[ev, n, 0], sdn.at[ev, n, 1])
 
-            @pl.when(n > 0)
-            def _():
-                forward(ev, n)
-
     def h_rest(ev):
-        @pl.loop(0, top)
+        h_inside(ev, 0)
+
+        @pl.loop(1, top, step=2)
         def _(z):
             h_inside(ev, z)
+            h_inside(ev, z + 1)
 
     def e_rest(ev, n):
-        @pl.loop(1, top)
+        @pl.loop(1, top, step=2)
         def _(z):
             e_layer(ev, n, z, below(ev, z))
+            e_layer(ev, n, z + 1, below(ev, z + 1))
 
     @pl.loop(0, 2 * STEPS - 2)
     def _(i):
@@ -420,11 +427,50 @@
 
         e_rest(ev, n)
 
+        @pl.when((i > 0) & (i < 2 * STEPS - 3))
+        def _():
+            forward(1 - ev, (i + 1) // 2)
+
         @pl.when(ev == 1)
         def _():
             @pl.loop(0, depth)
             def _(z):
                 add_total(n, z)
+
+    def settle():
+        @pl.loop(1, LINE)
+        def _(q):
+            gather_line(q, place).wait_send()
+
+        @pl.loop(1, COLUMNS)
+        def _(p):
+            sums_column(p, col_x).wait_send()
+
+            @pl.loop(0, LINE)
+            def _(which):
+                gather_column(p, col_x, which).wait_send()
+
+        @pl.loop(0, 2 * STEPS)
+        def _(i):
+            n, ev = i // 2, lax.rem(i, 2)
+
+            @pl.when(has_up)
+            def _():
+                u1(ev, n).wait_send()
+                u2(ev, n).wait_send()
+
+            @pl.when(has_dn)
+            def _():
+                d1(ev, n, sdn.at[ev, n, 0]).wait_send()
+                d2(ev, n, sdn.at[ev, n, 1]).wait_send()
+
+            @pl.when(relay_up)
+            def _():
+                relay_u2(ev, n).wait_send()
+
+            @pl.when(relay_dn)
+            def _():
+                relay_d2(ev, n).wait_send()
 
     n = STEPS - 1
 
@@ -433,6 +479,10 @@
         h_rest(ev)
         e_rest(ev, n)
 
+        @pl.when(ev == 0)
+        def _():
+            forward(0, n)
+
     @pl.loop(1, top)
     def _(z):
         add_total(n, z)
@@ -442,9 +492,10 @@
     def _(p):
         sums_column(p, col_x).start()
 
+    forward(1, n)
+
     @pl.loop(0, 2)
     def _(ev):
-        forward(ev, n)
         edges(ev, n, False)
 
         @pl.when(ev == 0)
@@ -462,6 +513,8 @@
             def _(q):
                 sums_line(q, place).start()
 
+            settle()
+
     add_total(n, 0)
     add_total(n, top)
     pack_sums(0, edge, 0, EDGE)
@@ -480,12 +533,13 @@
     for z in range(1, top):
         grad_ref[z * block_rows : (z + 1) * block_rows, :] = middle[(z - 1) * block_rows : z * block_rows]
 
-    def add_edge(d, acc):
-        sender = peer_of(d)
-        sums_edge(d, sender).wait_recv()
-        return acc + edge_in[rows_of(slot_of(sender), EDGE), :]
-
-    ends = lax.fori_loop(1, GROUPS, add_edge, edge[rows_of(slot_of(grp), EDGE), :])
+    others = pl.ds(0, (GROUPS - 1) * EDGE)
+    all_edges = peer_copy(edge.at[others, :], edge_in.at[others, :], se_s, se_r, peer_of(1))
+    edge_in[rows_of(slot_of(grp), EDGE), :] = edge[rows_of(slot_of(grp), EDGE), :]
+    all_edges.wait_recv()
+    ends = edge_in[0:EDGE, :]
+    for other in range(1, GROUPS):
+        ends = ends + edge_in[other * EDGE : (other + 1) * EDGE, :]
     grad_ref[0:block_rows, :] = ends[:block_rows]
     grad_ref[top * block_rows : depth * block_rows, :] = ends[block_rows:]
 
@@ -493,39 +547,9 @@
 
     @pl.loop(1, LINE)
     def _(q):
-        gather_line(q, place).wait_send()
         sums_line(q, place).wait_send()
 
-    @pl.loop(1, COLUMNS)
-    def _(p):
-        gather_column(p, col_x).wait_send()
-        sums_column(p, col_x).wait_send()
-
-    @pl.loop(1, GROUPS)
-    def _(d):
-        sums_edge(d, grp).wait_send()
-
-    @pl.loop(0, 2)
-    def _(ev):
-        @pl.loop(0, STEPS)
-        def _(n):
-            @pl.when(has_up)
-            def _():
-                u1(ev, n).wait_send()
-                u2(ev, n).wait_send()
-
-            @pl.when(has_dn)
-            def _():
-                d1(ev, n, sdn.at[ev, n, 0]).wait_send()
-                d2(ev, n, sdn.at[ev, n, 1]).wait_send()
-
-            @pl.when(relay_up)
-            def _():
-                relay_u2(ev, n).wait_send()
-
-            @pl.when(relay_dn)
-            def _():
-                relay_d2(ev, n).wait_send()
+    all_edges.wait_send()
 
 
 def per_device(
@@ -540,6 +564,9 @@
     hbm = pl.BlockSpec(memory_space=pltpu.HBM)
     dma = pltpu.SemaphoreType.DMA
     steps = dma((2, STEPS))
+    def in_hbm(a):
+        return pltpu.with_memory_space_constraint(a, pltpu.HBM)
+
     finals, grad = pl.pallas_call(
         evolve_kernel,
         out_shape=(jax.ShapeDtypeStruct(fwd_fields.shape, f32), jax.ShapeDtypeStruct((rows, width_y), f32)),
@@ -566,11 +593,11 @@
             pltpu.VMEM(layer, f32),
             *(pltpu.SMEM(a.shape, a.dtype) for a in (source_pos, wave_idx, block_ids, material_idx, material_eps)),
             dma((5,)), dma((2,)), dma(()), dma(()), *[steps] * 10,
-            *[dma((LINE,))] * 2, *[dma((COLUMNS,))] * 4, *[dma((LINE,))] * 2, *[dma((GROUPS,))] * 2,
+            *[dma((LINE,))] * 2, *[dma((COLUMNS, LINE))] * 2, *[dma((COLUMNS,))] * 2, *[dma((LINE,))] * 2, dma(()), dma(()),
         ],
         compiler_params=pltpu.CompilerParams(collective_id=0, has_side_effects=True, vmem_limit_bytes=48 << 20),
         name="evolve",
-    )(source_pos, wave_idx, block_ids, material_idx, material_eps, density.reshape(rows, width_y), fwd_fields, adj_fields)
+    )(in_hbm(source_pos), wave_idx, in_hbm(block_ids), in_hbm(material_idx), in_hbm(material_eps), in_hbm(density.reshape(rows, width_y)), fwd_fields, adj_fields)
     return finals, grad.reshape(density.shape)
 
 

time: 74.5 us -> 70.5 us (0.946)
  the two profiles are of different devices: /device:TPU:25 before, /device:TPU:1 now
where the time goes in v5:
time: 70.5 us; the launch traced here: 70.4 us
  Pallas kernels  66.8 us (95%)
  local copies, waits for them, and re-layouts  2.27 us (3%)
  between operations  1.29 us (2%)
    pallas_call x1, Pallas kernels, per_device(): pl.pallas_call(evolve_kernel, out_shape=(jax.ShapeDtypeStruct(fwd_fields....  66.8 us
    unnamed x2, local copies, waits for them, and re-layouts  2.27 us

profile of v5, /device:TPU:1, one launch (start us, length us, event | category | flops | bytes accessed | tf_op | source)
XLA Modules:
  0.0 70.4 jit_solution(6022972412508959345)
XLA Ops:
  1.3 66.8 %evolve.1 = (f32[1,6,8,128,128]{4,3,2,1,0:T(8,128)S(1)}, f32[32,128]{1,0:T(8,128)S(1)}) custom-call(s32[1,3]{1,0:T(1,128)} %pos_hbm.1, s32[1]{0:T(128)S(6)} %copy.12.wave_hbm, s32[32]{0:T(128)} %ids_hbm.1, s32[32]{0:T(128)} %mat_hbm.1, f32[4]{0:T(128)} %eps_hbm.1, f32[32,128]{1,0:T(8,128)} %bitcast.3, f32[1,6,8,128,128]{4,3,2,1,0:T(8,128)} %fwd_ref.1, ...), custom_call_target="tpu_custom_call" | custom-call | tf_op jit(solution)/shard_map/evolve/pallas_call | solution.py:570
  68.1 1.7 %copy.13 = f32[1,6,8,128,128]{4,3,2,1,0:T(8,128)} copy(f32[1,6,8,128,128]{4,3,2,1,0:T(8,128)S(1)} %get-tuple-element.8) | data formatting | bytes 6291456
  69.8 0.6 copy.14

commit v6 on v5

--- a/solution.py
+++ b/solution.py
@@ -19,6 +19,8 @@
 EDGE = 8
 LINE = 8
 COLUMNS = 4
+DIRECT = 128
+PIECE = 64
 
 
 def evolve_kernel(
@@ -37,9 +39,15 @@
     has_up, has_dn = slab < last, slab > 0
     run, col_x, core = grp // LINE, lax.rem(grp // 2, COLUMNS), lax.rem(grp, 2)
     place = run * 2 + core
+    middle_run = (run == 1) | (run == 2)
     far_low, far_high = slab == low, slab == high
     relay_up, relay_dn = slab == 0, slab == last
+    via_low, via_high = (far_low & middle_run, far_low), (far_high & middle_run, far_high)
+    up_relays, dn_relays = (relay_up & middle_run, relay_up), (relay_dn & middle_run, relay_dn)
     inner = pl.ds(PAD, width_x)
+    near = pl.ds(0, DIRECT)
+    fars = [pl.ds(DIRECT + p * PIECE, PIECE) for p in range(2)]
+    kept_rows = [pl.ds(p * PIECE, PIECE) for p in range(2)]
     fields = (fwd_ref, adj_ref)
 
     def copy_to(src, dst, send, recv, to_slab):
@@ -47,65 +55,81 @@
             src_ref=src, dst_ref=dst, send_sem=send, recv_sem=recv, device_id=(grp, to_slab), device_id_type=MESH)
 
     def u1(ev, n):
-        return copy_to(pout.at[ev, n, 0], pin.at[ev, n, 0], u1_s.at[ev, n], u1_r.at[ev, n], slab + 1)
-
-    def u2(ev, n):
-        return copy_to(pout.at[ev, n, 1], pin.at[ev, n, 1], u2_s.at[ev, n], u2_r.at[ev, n], slab + 1)
-
-    def u2_via(ev, n):
-        return copy_to(pout.at[ev, n, 1], rel.at[ev, n], u2_s.at[ev, n], rl_r.at[ev, n], 0)
-
-    def relay_u2(ev, n):
-        return copy_to(rel.at[ev, n], pin.at[ev, n, 1], rl_s.at[ev, n], u2_r.at[ev, n], high)
+        return copy_to(pout.at[ev, n, near, :], pin.at[ev, n, near, :], u1_s.at[ev, n], u1_r.at[ev, n], slab + 1)
+
+    def u2(ev, n, p):
+        return copy_to(pout.at[ev, n, fars[p], :], pin.at[ev, n, fars[p], :], u2_s.at[ev, n, p], u2_r.at[ev, n, p], slab + 1)
+
+    def u2_via(ev, n, p):
+        return copy_to(pout.at[ev, n, fars[p], :], rel.at[ev, n, kept_rows[p], :], u2_s.at[ev, n, p], rl_r.at[ev, n, p], 0)
+
+    def relay_u2(ev, n, p):
+        return copy_to(rel.at[ev, n, kept_rows[p], :], pin.at[ev, n, fars[p], :], rl_s.at[ev, n, p], u2_r.at[ev, n, p], high)
 
     def d1(ev, n, src):
-        return copy_to(src, eu.at[ev, n, 0], d1_s.at[ev, n], d1_r.at[ev, n], slab - 1)
-
-    def d2(ev, n, src):
-        return copy_to(src, eu.at[ev, n, 1], d2_s.at[ev, n], d2_r.at[ev, n], slab - 1)
-
-    def d2_via(ev, n, src):
-        return copy_to(src, rel.at[ev, n], d2_s.at[ev, n], rl_r.at[ev, n], last)
-
-    def relay_d2(ev, n):
-        return copy_to(rel.at[ev, n], eu.at[ev, n, 1], rl_s.at[ev, n], d2_r.at[ev, n], low)
+        return copy_to(src, eu.at[ev, n, near, :], d1_s.at[ev, n], d1_r.at[ev, n], slab - 1)
+
+    def d2(ev, n, p, src):
+        return copy_to(src, eu.at[ev, n, fars[p], :], d2_s.at[ev, n, p], d2_r.at[ev, n, p], slab - 1)
+
+    def d2_via(ev, n, p, src):
+        return copy_to(src, rel.at[ev, n, kept_rows[p], :], d2_s.at[ev, n, p], rl_r.at[ev, n, p], last)
+
+    def relay_d2(ev, n, p):
+        return copy_to(rel.at[ev, n, kept_rows[p], :], eu.at[ev, n, fars[p], :], rl_s.at[ev, n, p], d2_r.at[ev, n, p], low)
 
     def send_up(ev, n):
         @pl.when(has_up)
         def _():
-            @pl.when(far_low)
+            for p in (1, 0):
+
+                @pl.when(via_low[p])
+                def _():
+                    u2_via(ev, n, p).start()
+
+                @pl.when(jnp.logical_not(via_low[p]))
+                def _():
+                    u2(ev, n, p).start()
+
+            u1(ev, n).start()
+
+    def send_far_dn(ev, n, srcs):
+        for p in (1, 0):
+
+            @pl.when(via_high[p])
             def _():
-                u2_via(ev, n).start()
-
-            @pl.when(jnp.logical_not(far_low))
+                d2_via(ev, n, p, srcs[p]).start()
+
+            @pl.when(jnp.logical_not(via_high[p]))
             def _():
-                u2(ev, n).start()
-
-            u1(ev, n).start()
-
-    def send_dn(ev, n, first, second):
+                d2(ev, n, p, srcs[p]).start()
+
+    def send_dn(ev, n):
         @pl.when(has_dn)
         def _():
-            @pl.when(far_high)
+            send_far_dn(ev, n, [sdn.at[ev, n - 1, rows, :] for rows in fars])
+            d1(ev, n, sdn.at[ev, n - 1, near, :]).start()
+
+    def send_dn_first(ev):
+        f = fields[ev]
+
+        @pl.when(has_dn)
+        def _():
+            send_far_dn(ev, 0, [f.at[0, 1, 0, rows, :] for rows in kept_rows])
+            d1(ev, 0, f.at[0, 0, 0]).start()
+
+    def forward(ev, n):
+        for p in (1, 0):
+
+            @pl.when(up_relays[p])
             def _():
-                d2_via(ev, n, second).start()
-
-            @pl.when(jnp.logical_not(far_high))
+                u2_via(ev, n, p).wait_recv()
+                relay_u2(ev, n, p).start()
+
+            @pl.when(dn_relays[p])
             def _():
-                d2(ev, n, second).start()
-
-            d1(ev, n, first).start()
-
-    def forward(ev, n):
-        @pl.when(relay_up)
-        def _():
-            u2_via(ev, n).wait_recv()
-            relay_u2(ev, n).start()
-
-        @pl.when(relay_dn)
-        def _():
-            d2_via(ev, n, rel.at[ev, n]).wait_recv()
-            relay_d2(ev, n).start()
+                d2_via(ev, n, p, rel.at[ev, n, kept_rows[p], :]).wait_recv()
+                relay_d2(ev, n, p).start()
 
     def peer_copy(src, dst, send, recv, peer):
         return pltpu.make_async_remote_copy(
@@ -257,16 +281,16 @@
             ahead = pl.ds(PAD + r + 1, ROWS)
             ex, ey, ez = (st[ev, c, top, here, :] for c in range(3))
             out = pl.ds(r, ROWS)
-            pout[ev, n, 0, out, :] = st[ev, 3, top, here, :] - COURANT * ((next_y(ez) - ez) + ey)
-            pout[ev, n, 1, out, :] = st[ev, 4, top, here, :] + COURANT * ((st[ev, 2, top, ahead, :] - ez) + ex)
+            pout[ev, n, pl.ds(0 * width_x + r, ROWS), :] = st[ev, 3, top, here, :] - COURANT * ((next_y(ez) - ez) + ey)
+            pout[ev, n, pl.ds(1 * width_x + r, ROWS), :] = st[ev, 4, top, here, :] + COURANT * ((st[ev, 2, top, ahead, :] - ez) + ex)
 
     def h_top(ev, n):
         for r, here in chunks():
             ahead = pl.ds(PAD + r + 1, ROWS)
             out = pl.ds(r, ROWS)
             ex, ey = (st[ev, c, top, here, :] for c in range(2))
-            st[ev, 3, top, here, :] = pout[ev, n, 0, out, :] + COURANT * eu[ev, n, 1, out, :]
-            st[ev, 4, top, here, :] = pout[ev, n, 1, out, :] - COURANT * eu[ev, n, 0, out, :]
+            st[ev, 3, top, here, :] = pout[ev, n, pl.ds(0 * width_x + r, ROWS), :] + COURANT * eu[ev, n, pl.ds(1 * width_x + r, ROWS), :]
+            st[ev, 4, top, here, :] = pout[ev, n, pl.ds(1 * width_x + r, ROWS), :] - COURANT * eu[ev, n, pl.ds(0 * width_x + r, ROWS), :]
             st[ev, 5, top, here, :] += -COURANT * ((st[ev, 1, top, ahead, :] - ey) - (next_y(ex) - ex))
 
     for ev in range(2):
@@ -283,7 +307,7 @@
     def _(p):
         gather_column(p, col_x, place, dens_ref).start()
 
-    send_dn(0, 0, fwd_ref.at[0, 0, 0], fwd_ref.at[0, 1, 0])
+    send_dn_first(0)
     send_up(0, 0)
 
     def e_layer(ev, n, z, below, send=None):
@@ -301,8 +325,8 @@
             for c, v in enumerate((ex, ey, ez)):
                 st[ev, c, z, here, :] = v
             if send is not None:
-                for c in range(send.shape[0]):
-                    send[c, out, :] = (ex, ey, ez)[c]
+                for c in range(2):
+                    send[pl.ds(c * width_x + r, ROWS), :] = (ex, ey, ez)[c]
 
     def filter_y(v):
         left = jnp.where(col == 0, 0.0, pltpu.roll(v, 1, axis=1))
@@ -338,7 +362,7 @@
             def _(p):
                 gather_column(p, col_x, which).start()
 
-        send_dn(1, 0, adj_ref.at[0, 0, 0], adj_ref.at[0, 1, 0])
+        send_dn_first(1)
         send_up(1, 0)
         forward(0, 0)
         forward(1, 0)
@@ -367,15 +391,16 @@
     def below_first(ev, n):
         def values(r):
             out, here = pl.ds(r, ROWS), pl.ds(PAD + r, ROWS)
-            return (pin[ev, n, 0, out, :] + half * st[ev, 1, 0, here, :], pin[ev, n, 1, out, :] - half * st[ev, 0, 0, here, :])
+            return (pin[ev, n, pl.ds(0 * width_x + r, ROWS), :] + half * st[ev, 1, 0, here, :], pin[ev, n, pl.ds(1 * width_x + r, ROWS), :] - half * st[ev, 0, 0, here, :])
 
         return values
 
     def edges(ev, n, sending):
         @pl.when(has_up)
         def _():
-            d1(ev, n, sdn.at[ev, n, 0]).wait_recv()
-            d2(ev, n, sdn.at[ev, n, 1]).wait_recv()
+            d1(ev, n, sdn.at[ev, n, near, :]).wait_recv()
+            for p in range(2):
+                d2(ev, n, p, sdn.at[ev, n, fars[p], :]).wait_recv()
 
         h_top(ev, n)
         e_layer(ev, n, top, below(ev, top))
@@ -386,11 +411,12 @@
         @pl.when(has_dn)
         def _():
             u1(ev, n).wait_recv()
-            u2(ev, n).wait_recv()
+            for p in range(2):
+                u2(ev, n, p).wait_recv()
 
         e_layer(ev, n, 0, below_first(ev, n), sdn.at[ev, n])
         if sending:
-            send_dn(ev, n + 1, sdn.at[ev, n, 0], sdn.at[ev, n, 1])
+            send_dn(ev, n + 1)
 
     def h_rest(ev):
         h_inside(ev, 0)
@@ -457,20 +483,24 @@
             @pl.when(has_up)
             def _():
                 u1(ev, n).wait_send()
-                u2(ev, n).wait_send()
+                for p in range(2):
+                    u2(ev, n, p).wait_send()
 
             @pl.when(has_dn)
             def _():
-                d1(ev, n, sdn.at[ev, n, 0]).wait_send()
-                d2(ev, n, sdn.at[ev, n, 1]).wait_send()
-
-            @pl.when(relay_up)
-            def _():
-                relay_u2(ev, n).wait_send()
-
-            @pl.when(relay_dn)
-            def _():
-                relay_d2(ev, n).wait_send()
+                d1(ev, n, sdn.at[ev, n, near, :]).wait_send()
+                for p in range(2):
+                    d2(ev, n, p, sdn.at[ev, n, fars[p], :]).wait_send()
+
+            for p in range(2):
+
+                @pl.when(up_relays[p])
+                def _():
+                    relay_u2(ev, n, p).wait_send()
+
+                @pl.when(dn_relays[p])
+                def _():
+                    relay_d2(ev, n, p).wait_send()
 
     n = STEPS - 1
 
@@ -502,19 +532,6 @@
         def _():
             pltpu.make_async_copy(st.at[0, :, :, inner, :], out_ref.at[0], store_sem).start()
 
-            @pl.loop(1, COLUMNS)
-            def _(p):
-                sender = column_peer(p)[0]
-                sums_column(p, sender).wait_recv()
-                kept = rows_of(col_x, LINE * INNER)
-                mine[kept, :] += column[rows_of(sender, LINE * INNER), :]
-
-            @pl.loop(1, LINE)
-            def _(q):
-                sums_line(q, place).start()
-
-            settle()
-
     add_total(n, 0)
     add_total(n, top)
     pack_sums(0, edge, 0, EDGE)
@@ -523,6 +540,19 @@
     @pl.loop(1, GROUPS)
     def _(d):
         sums_edge(d, grp).start()
+
+    @pl.loop(1, COLUMNS)
+    def _(p):
+        sender = column_peer(p)[0]
+        sums_column(p, sender).wait_recv()
+        kept = rows_of(col_x, LINE * INNER)
+        mine[kept, :] += column[rows_of(sender, LINE * INNER), :]
+
+    @pl.loop(1, LINE)
+    def _(q):
+        sums_line(q, place).start()
+
+    settle()
 
     def add_line(q, acc):
         sender = line_peer(q)[0]
@@ -563,7 +593,7 @@
     anywhere = pl.BlockSpec(memory_space=pl.ANY)
     hbm = pl.BlockSpec(memory_space=pltpu.HBM)
     dma = pltpu.SemaphoreType.DMA
-    steps = dma((2, STEPS))
+    steps, pieces = dma((2, STEPS)), dma((2, STEPS, 2))
     def in_hbm(a):
         return pltpu.with_memory_space_constraint(a, pltpu.HBM)
 
@@ -576,11 +606,8 @@
             pltpu.VMEM((2, 6, depth, width_x + 2 * PAD, width_y), f32),
             pltpu.VMEM((depth, *layer), f32),
             pltpu.VMEM((depth, *layer), f32),
-            pltpu.VMEM((2, STEPS, 2, *layer), f32),
-            pltpu.VMEM((2, STEPS, 2, *layer), f32),
-            pltpu.VMEM((2, STEPS, 2, *layer), f32),
-            pltpu.VMEM((2, STEPS, 2, *layer), f32),
-            pltpu.VMEM((2, STEPS, *layer), f32),
+            *[pltpu.VMEM((2, STEPS, 2 * width_x, width_y), f32)] * 4,
+            pltpu.VMEM((2, STEPS, 2 * width_x - DIRECT, width_y), f32),
             pltpu.VMEM((STEPS, *layer), f32),
             pltpu.VMEM((GROUPS * OWN, width_y), f32),
             pltpu.VMEM((GROUPS * INNER, width_y), f32),
@@ -592,7 +619,7 @@
             pltpu.VMEM((width_x, 2 * width_x), jnp.bfloat16),
             pltpu.VMEM(layer, f32),
             *(pltpu.SMEM(a.shape, a.dtype) for a in (source_pos, wave_idx, block_ids, material_idx, material_eps)),
-            dma((5,)), dma((2,)), dma(()), dma(()), *[steps] * 10,
+            dma((5,)), dma((2,)), dma(()), dma(()), steps, steps, pieces, pieces, steps, steps, pieces, pieces, pieces, pieces,
             *[dma((LINE,))] * 2, *[dma((COLUMNS, LINE))] * 2, *[dma((COLUMNS,))] * 2, *[dma((LINE,))] * 2, dma(()), dma(()),
         ],
         compiler_params=pltpu.CompilerParams(collective_id=0, has_side_effects=True, vmem_limit_bytes=48 << 20),

time: 70.5 us -> 66.9 us (0.949)
  the two profiles are of different devices: /device:TPU:1 before, /device:TPU:25 now
where the time goes in v6:
time: 66.9 us; the launch traced here: 66.8 us
  Pallas kernels  63.2 us (94%)
  local copies, waits for them, and re-layouts  2.27 us (3%)
  between operations  1.29 us (2%)
    pallas_call x1, Pallas kernels, per_device(): pl.pallas_call(evolve_kernel, out_shape=(jax.ShapeDtypeStruct(fwd_fields....  63.2 us
    unnamed x2, local copies, waits for them, and re-layouts  2.27 us

profile of v6, /device:TPU:25, one launch (start us, length us, event | category | flops | bytes accessed | tf_op | source)
XLA Modules:
  0.0 66.8 jit_solution(5298232569052593782)
XLA Ops:
  1.3 63.2 %evolve.1 = (f32[1,6,8,128,128]{4,3,2,1,0:T(8,128)S(1)}, f32[32,128]{1,0:T(8,128)S(1)}) custom-call(s32[1,3]{1,0:T(1,128)} %pos_hbm.1, s32[1]{0:T(128)S(6)} %copy.12.wave_hbm, s32[32]{0:T(128)} %ids_hbm.1, s32[32]{0:T(128)} %mat_hbm.1, f32[4]{0:T(128)} %eps_hbm.1, f32[32,128]{1,0:T(8,128)} %bitcast.3, f32[1,6,8,128,128]{4,3,2,1,0:T(8,128)} %fwd_ref.1, ...), custom_call_target="tpu_custom_call" | custom-call | tf_op jit(solution)/shard_map/evolve/pallas_call | solution.py:600
  64.5 1.7 %copy.13 = f32[1,6,8,128,128]{4,3,2,1,0:T(8,128)} copy(f32[1,6,8,128,128]{4,3,2,1,0:T(8,128)S(1)} %get-tuple-element.8) | data formatting | bytes 6291456
  66.2 0.6 copy.14
